TPU v7x, 128 devices: a whole 4x4x4 slice. The times are simulated.
128 devices in a mesh: branch: 4 (over x), seq: 32 (over z, y, core).
Axes of the slice: x: 4, y: 4, z: 4, core: 2. Of those that a mesh axis runs over, the one named last changes fastest.
Arguments:
- query: bfloat16 [4, 4096, 8192], P('branch', 'seq'), may hold values from -150 to 150
- key_new: bfloat16 [4, 4096, 1024], P('branch', 'seq'), may hold values from -6 to 6
- value_new: bfloat16 [4, 4096, 1024], P('branch', 'seq'), may hold values from -18 to 18
- hist_key: bfloat16 [512, 1024], P('seq'), may hold values from -6 to 6
- hist_value: bfloat16 [512, 1024], P('seq'), may hold values from -18 to 18
- sib_source: int32 [4, 4], replicated, may hold values from 0 to 3, as said below
- sib_block: int32 [4, 4], replicated, may hold values from 0 to 15, as said below
- sib_mask: int32 [4, 16, 4], replicated, may hold values 0 or 1
Outputs:
- attended: bfloat16 [4, 4096, 8192], P('branch', 'seq')
Inputs may be any that keep to these rules, and one draw needn't show every extreme that they name: `sib_source`: never the reader itself. In every reader's list exactly 2 slots name one source and no source is named more than 2 times. `sib_block`: A reader lists no block of one source twice.
All inputs are finite; a program needn't handle non-finite values.
Results may differ from a plain program's by a relative error of at most 0.0036.
Values may be sent and summed in bfloat16 or wider, within the bound.
No kernel may reach another device: no remote copies, remote signals or barrier semaphores. Data moves between devices by JAX's collectives and lax.ppermute only.
A program may use at most 128 MiB of HBM per device.

v0:
```python
import math

import jax
import jax.numpy as jnp
from jax import lax
from jax.experimental import pallas as pl
from jax.experimental.pallas import tpu as pltpu
from jax.sharding import Mesh
from jax.sharding import PartitionSpec as P


KVH = 8
HD = 128
NSIB = 4
SRCMAX = 2
TOK = 128
PAST = 16
GROUP = 1024
Z, Y, CORE = "seq_0", "seq_1", "seq_2"
EXP2_SCALE = math.log2(math.e) / math.sqrt(HD)
HIDDEN = -1e30
OWN0, SIB0, DUMMY = 4, 36, 44
VROWS = HD + 16
SPAN = 8
QW = 512
HALVES = GROUP // QW
KB = SPAN * TOK


def make_kernel(kind, chunks):
    has_own, has_sib = kind != "close", kind != "open"

    def kernel(plan, *refs):
        refs = list(refs)

        def take(count):
            taken = refs[:count]
            del refs[:count]
            return taken

        queries = take(chunks)
        states = take(chunks) if kind == "close" else []
        owns = take(4) if has_own else []
        sibs = take(1) if has_sib else []
        outs = take(chunks)
        kbuf, vbuf, past, todo, q_t, s_buf, p_buf, a_buf, acc, top, sem = refs
        step = pl.program_id(0)
        chunk_z, chunk_core, y = plan[0, step], plan[1, step], plan[2, step]

        @pl.when(step == 0)
        def _():
            pairs = []
            for r, own in enumerate(owns):
                here = pl.ds(OWN0 + 8 * r, 8)
                pairs.append((own.at[:, pl.ds(0, TOK)], kbuf.at[here]))
                pairs.append((own.at[:, pl.ds(TOK, HD)], vbuf.at[here, pl.ds(0, HD)]))
                pairs.append((own.at[:, pl.ds(TOK + HD, 2 * PAST)], past.at[r]))
            for t in range(4 if has_sib else 0):
                source = sibs[0].at[lax.rem(y + 4 - t, 4)]
                here = pl.ds(SIB0 + 4 * (t % 2), 4)
                pairs.append((source, kbuf.at[here] if t < 2 else vbuf.at[here, pl.ds(0, HD)]))
            copies = [pltpu.make_async_copy(a, b, sem.at[i]) for i, (a, b) in enumerate(pairs)]
            for copy in copies:
                copy.start()
            row = lax.broadcasted_iota(jnp.int32, (VROWS - HD, TOK), 0)
            ones = jnp.where(row == 0, 1.0, 0.0).astype(jnp.bfloat16)
            for t in range(DUMMY):
                vbuf[t, HD:VROWS, :] = ones
            vbuf[DUMMY] = jnp.zeros((VROWS, TOK), jnp.bfloat16)
            for copy in copies:
                copy.wait()
            for r in range(len(owns)):
                kbuf[r] = past[r, :, 0:PAST].reshape(TOK, HD)
                vbuf[r, 0:HD] = past[r, :, PAST : 2 * PAST].reshape(TOK, HD).T

        def load(ref):
            for h in range(KVH):
                cols = slice(h * HD, (h + 1) * HD)
                scaled = ref[:, cols].T.astype(jnp.float32) * EXP2_SCALE
                upper = scaled.astype(jnp.bfloat16)
                q_t[0:HD, cols] = upper
                q_t[HD : 2 * HD, cols] = (scaled - upper.astype(jnp.float32)).astype(jnp.bfloat16)

        for i in range(chunks):

            @pl.when(step == i)
            def _(i=i):
                load(queries[i])
                if kind == "close":
                    acc[...] = states[i][0:VROWS]
                    top[...] = states[i][VROWS : VROWS + 1]

        n = jnp.int32(0)
        if has_own:
            todo[0] = OWN0 + 2 * chunk_z + chunk_core
            for t in range(4):
                todo[1 + t] = t

            def earlier(z, n):
                for r in range(4):
                    todo[n + 2 * r] = OWN0 + 8 * r + 2 * z
                    todo[n + 2 * r + 1] = OWN0 + 8 * r + 2 * z + 1
                return n + 8

            n = lax.fori_loop(0, chunk_z, earlier, jnp.int32(5))
            todo[n] = OWN0 + 2 * chunk_z
            n = n + chunk_core
            for r in range(1, 4):
                todo[n] = OWN0 + 8 * r + 2 * chunk_z
                todo[n + 1] = OWN0 + 8 * r + 2 * chunk_z + 1
                n = n + jnp.where(y >= r, 2, 0)
        if has_sib:
            for slot in range(NSIB):
                todo[n] = SIB0 + slot
                todo[n + 1] = SIB0 + 4 + slot
                n = n + jnp.where(plan[3 + slot, step] == 1, 2, 0)
        repeat = todo[1 if has_own else 0]
        for t in range(2 * SPAN):
            todo[n + t] = DUMMY
        kbuf[DUMMY] = kbuf[repeat]
        groups = lax.div(n + SPAN - 1, SPAN)

        def score(j, g):
            keys = jnp.concatenate([kbuf[todo[j * SPAN + t]] for t in range(SPAN)], axis=0)
            s_buf[g] = lax.dot_general(
                jnp.concatenate([keys, keys], axis=1),
                q_t[:, g * QW : (g + 1) * QW],
                (((1,), (0,)), ((), ())),
                preferred_element_type=jnp.float32,
            )

        def weigh(g, first=False):
            cols = slice(g * QW, (g + 1) * QW)
            s = s_buf[g]
            if first:
                key = lax.broadcasted_iota(jnp.int32, (TOK, QW), 0)
                token = lax.broadcasted_iota(jnp.int32, (TOK, QW), 1) % TOK
                s = jnp.concatenate([jnp.where(key <= token, s[0:TOK], HIDDEN), s[TOK:]], axis=0)
            peak = jnp.max(s, axis=0, keepdims=True)
            if not first:
                before = top[:, cols]
                peak = jnp.maximum(before, peak)
                a_buf[:, cols] = jnp.exp2(before - peak)
            top[:, cols] = peak
            p_buf[g] = jnp.exp2(s - peak).astype(jnp.bfloat16)

        def gather(j, g, first=False):
            cols = slice(g * QW, (g + 1) * QW)
            values_t = jnp.concatenate([vbuf[todo[j * SPAN + t]] for t in range(SPAN)], axis=1)
            part = lax.dot_general(
                values_t, p_buf[g], (((1,), (0,)), ((), ())), preferred_element_type=jnp.float32
            )
            acc[:, cols] = part if first else acc[:, cols] * a_buf[:, cols] + part

        last = HALVES - 1

        def turn(j, carry):
            for g in range(HALVES):
                if g == 0:
                    gather(j - 1, last)
                else:
                    gather(j, g - 1)
                weigh(g)
                if g < last:
                    score(j, g + 1)
                else:
                    score(j + 1, 0)
            return carry

        if has_own:
            score(0, 0)
            for g in range(HALVES):
                if g < last:
                    score(0, g + 1)
                else:
                    score(1, 0)
                if g:
                    gather(0, g - 1, first=True)
                weigh(g, first=True)
            acc[:, last * QW :] = jnp.zeros((VROWS, QW), jnp.float32)
            a_buf[:, last * QW :] = jnp.ones((1, QW), jnp.float32)
            lax.fori_loop(1, groups, turn, 0)
            gather(groups - 1, last)
        else:
            @pl.when(groups > 0)
            def _():
                for g in range(HALVES):
                    score(0, g)
                for g in range(HALVES):
                    weigh(g)
                    gather(0, g)

        def store(ref):
            if kind == "open":
                ref[0:VROWS] = acc[...]
                ref[VROWS:] = jnp.broadcast_to(top[...], (8, GROUP))
                return
            for h in range(KVH):
                cols = slice(h * HD, (h + 1) * HD)
                ref[:, cols] = (acc[0:HD, cols] / acc[HD : HD + 1, cols]).T.astype(jnp.bfloat16)

        for i in range(chunks):

            @pl.when(step == i)
            def _(i=i):
                store(outs[i])

    return kernel


def attend(kind, plan, queries, states, owns, sib):
    chunks = len(queries)

    def whole(a):
        return pl.BlockSpec(a.shape, lambda i, plan: (0,) * a.ndim, pipeline_mode=pl.Buffered(1))

    blocked = [*queries, *(states if kind == "close" else ())]
    raw = [*(owns if kind != "close" else ()), *((sib,) if kind != "open" else ())]
    if kind == "open":
        result = jax.ShapeDtypeStruct((VROWS + 8, GROUP), jnp.float32)
    else:
        result = jax.ShapeDtypeStruct((TOK, GROUP), jnp.bfloat16)
    return pl.pallas_call(
        make_kernel(kind, chunks),
        out_shape=(result,) * chunks,
        grid_spec=pltpu.PrefetchScalarGridSpec(
            num_scalar_prefetch=1,
            grid=(chunks,),
            in_specs=[whole(a) for a in blocked] + [pl.BlockSpec(memory_space=pl.ANY)] * len(raw),
            out_specs=[pl.BlockSpec(result.shape, lambda i, plan: (0, 0))] * chunks,
            scratch_shapes=[
                pltpu.VMEM((DUMMY + 1, TOK, HD), jnp.bfloat16),
                pltpu.VMEM((DUMMY + 1, VROWS, TOK), jnp.bfloat16),
                pltpu.VMEM((4, 8, 2 * PAST, HD), jnp.bfloat16),
                pltpu.SMEM((72,), jnp.int32),
                pltpu.VMEM((2 * HD, GROUP), jnp.bfloat16),
                pltpu.VMEM((HALVES, KB, QW), jnp.float32),
                pltpu.VMEM((HALVES, KB, QW), jnp.bfloat16),
                pltpu.VMEM((1, GROUP), jnp.float32),
                pltpu.VMEM((VROWS, GROUP), jnp.float32),
                pltpu.VMEM((1, GROUP), jnp.float32),
                pltpu.SemaphoreType.DMA((16,)),
            ],
        ),
        compiler_params=pltpu.CompilerParams(vmem_limit_bytes=32 * 2**20),
    )(plan, *blocked, *raw)


def shifted(value, axis, by):
    n = lax.axis_size(axis)
    return lax.ppermute(value, axis, [(k, (k + by) % n) for k in range(n)])


def exchanged(value, step):
    return lax.ppermute(value, (Z, CORE), [(k, k ^ step) for k in range(8)])


def after(value, *others):
    return lax.optimization_barrier((value, *others))[0]


def packing(key_ref, value_ref, past_key_ref, past_value_ref, out_ref):
    for h in range(KVH):
        cols = slice(h * HD, (h + 1) * HD)
        out_ref[h, 0:TOK] = key_ref[0, :, cols]
        out_ref[h, TOK : TOK + HD] = value_ref[0, :, cols].T
        out_ref[h, TOK + HD : TOK + HD + PAST] = past_key_ref[:, cols]
        out_ref[h, TOK + HD + PAST :] = past_value_ref[:, cols]


def packed(*arrays):
    shape = jax.ShapeDtypeStruct((KVH, TOK + HD + 2 * PAST, HD), jnp.bfloat16)
    return pl.pallas_call(packing, out_shape=shape, name="packing")(*arrays)


def attention(query, key_new, value_new, hist_key, hist_value, sib_source, sib_block, sib_mask):
    z, y, core = lax.axis_index(Z), lax.axis_index(Y), lax.axis_index(CORE)
    me = z * 2 + core
    reader = lax.axis_index("branch")

    send = packed(key_new, value_new, hist_key, hist_value)
    own = lax.all_to_all(send, (Z, CORE), split_axis=0, concat_axis=0, tiled=True)
    up, down = shifted(own, Y, 1), shifted(own, Y, -1)
    onward = shifted(up[:4], Y, 1), shifted(down[4:], Y, -1)
    over = jnp.concatenate(onward, axis=0)
    owns = (own, up, over, down)

    cols = after(query[0], own)
    queries = {}
    for s in QORDER:
        piece = lax.dynamic_slice_in_dim(cols, (me ^ s) * GROUP, GROUP, 1)
        queries[s] = exchanged(piece, s) if s else piece

    start = TOK * (y // 2)
    mine = jnp.concatenate(
        [
            lax.dynamic_slice(o.reshape(4, 2, -1, HD), (0, y % 2, start, 0), (4, 1, TOK, HD)).reshape(4, TOK, HD)
            for o in owns
        ]
    )
    my_source = lax.dynamic_index_in_dim(sib_source, reader, 0, keepdims=False)
    my_mask = lax.dynamic_index_in_dim(sib_mask, reader, 0, keepdims=False)
    from_me = sib_source == reader
    sender_rank = jnp.cumsum(from_me.astype(jnp.int32), axis=1) - 1
    slot_hit = from_me[:, :, None] & (
        sender_rank[:, :, None] == jnp.arange(SRCMAX, dtype=jnp.int32)[None, None, :]
    )
    send_table = jnp.sum(jnp.where(slot_hit, sib_block[:, :, None], 0), axis=1)
    place = ((y - send_table) % 4) * 4 + send_table // 4
    got = lax.all_to_all(mine[place], "branch", split_axis=0, concat_axis=0, tiled=True)
    slots = jnp.arange(NSIB, dtype=jnp.int32)
    same = (my_source[None, :] == my_source[:, None]) & (slots[None, :] < slots[:, None])
    rank = jnp.sum(same.astype(jnp.int32), axis=1)
    listed = got.reshape(-1, HD, HD)[my_source * SRCMAX + rank]
    sib = jnp.stack([listed, shifted(listed, Y, 1), shifted(listed, Y, 2), shifted(listed, Y, -1)])

    def plan_of(steps):
        chunks = jnp.stack([me ^ s for s in steps])
        visible = my_mask[(chunks // 2) * 4 + y]
        rows = [(chunks // 2)[None], (chunks % 2)[None], jnp.broadcast_to(y, (1, len(steps))), visible.T]
        return jnp.concatenate(rows, axis=0).astype(jnp.int32)

    parts, states, previous = {}, {}, None
    for kind, steps in CALLS:
        asked = [queries[s] for s in steps]
        if previous is not None:
            asked[0] = after(asked[0], previous)
        results = attend(kind, plan_of(steps), asked, [states.get(s) for s in steps], owns, sib)
        previous = results[0]
        for s, result in zip(steps, results):
            if kind == "open":
                states[s] = result
            else:
                parts[s] = exchanged(result, s) if s else result
    out = jnp.zeros((TOK, KVH * GROUP), jnp.bfloat16)
    for s in range(8):
        out = lax.dynamic_update_slice_in_dim(out, parts[s], (me ^ s) * GROUP, 1)
    return out[None]


QORDER = (2, 3, 4, 5, 6, 7, 1, 0)
CALLS = (("open", (2, 3)), ("full", (4, 5)), ("close", (2, 3)), ("full", (6, 7)), ("full", (1, 0)))


def solution(mesh):
    split = Mesh(mesh.devices.reshape(mesh.shape["branch"], 4, 4, 2), ("branch", Z, Y, CORE))
    seq = (Z, Y, CORE)
    placed = (
        P("branch", seq, None),
        P("branch", seq, None),
        P("branch", seq, None),
        P(seq, None),
        P(seq, None),
        P(),
        P(),
        P(),
    )
    return jax.shard_map(
        attention, mesh=split, in_specs=placed, out_specs=P("branch", seq, None), check_vma=False
    )
```

profile of v0, /device:TPU:31, one launch (start us, length us, event | category | flops | bytes accessed | tf_op | source)
XLA Modules:
  0.0 172.8 jit_solution(15519790691275666330)
XLA Ops:
  0.0 2.0 %packing.1 = bf16[8,288,128]{2,1,0:T(8,128)(2,1)} custom-call(bf16[1,128,1024]{2,1,0:T(8,128)(2,1)} %key_ref.1, bf16[1,128,1024]{2,1,0:T(8,128)(2,1)} %value_ref.1, bf16[16,1024]{1,0:T(8,128)(2,1)} %past_key_ref.1, bf16[16,1024]{1,0:T(8,128)(2,1)} %past_value_ref.1), custom_call_target="tpu_custom_call" | custom-call | tf_op jit(solution)/shard_map/packing/pallas_call | solution.py:273
  2.0 6.0 %all-to-all-start = ((bf16[8,288,128]{2,1,0:T(8,128)(2,1)}), bf16[8,288,128]{2,1,0:T(8,128)(2,1)S(1)}, u32[]{:S(2)}, u32[]{:S(2)}) async-start(bf16[8,288,128]{2,1,0:T(8,128)(2,1)} %packing.1), calls=%async_computation | async-start | bytes 1179648 | tf_op jit(solution)/shard_map/all_to_all | solution.py:282
  9.0 9.0 %all-to-all-done.refs_2_ = bf16[8,288,128]{2,1,0:T(8,128)(2,1)S(1)} async-done(((bf16[8,288,128]{2,1,0:T(8,128)(2,1)}), bf16[8,288,128]{2,1,0:T(8,128)(2,1)S(1)}, u32[]{:S(2)}, u32[]{:S(2)}) %all-to-all-start) | async-done | bytes 589856 | tf_op jit(solution)/shard_map/all_to_all | solution.py:282
  18.1 1.5 collective-permute-start.7
  21.5 10.4 %collective-permute-done.5.refs_3_ = bf16[8,288,128]{2,1,0:T(8,128)(2,1)S(1)} collective-permute-done((bf16[8,288,128]{2,1,0:T(8,128)(2,1)S(1)}, bf16[8,288,128]{2,1,0:T(8,128)(2,1)S(1)}, u32[]{:S(2)}, u32[]{:S(2)}) %collective-permute-start.5) | collective-permute-done | bytes 589856 | tf_op jit(solution)/shard_map/ppermute | solution.py:251
  32.0 1.3 collective-permute-start.6
  33.7 5.1 %collective-permute-done.6 = bf16[4,288,128]{2,1,0:T(8,128)(2,1)S(1)} collective-permute-done((bf16[4,288,128]{2,1,0:T(8,128)(2,1)S(1)}, bf16[4,288,128]{2,1,0:T(8,128)(2,1)S(1)}, u32[]{:S(2)}, u32[]{:S(2)}) %collective-permute-start.6) | collective-permute-done | bytes 294944 | tf_op jit(solution)/shard_map/ppermute | solution.py:251
  38.8 2.4 %collective-permute-done.8 = bf16[4,288,128]{2,1,0:T(8,128)(2,1)S(1)} collective-permute-done((bf16[4,288,128]{2,1,0:T(8,128)(2,1)S(1)}, bf16[4,288,128]{2,1,0:T(8,128)(2,1)S(1)}, u32[]{:S(2)}, u32[]{:S(2)}) %collective-permute-start.8) | collective-permute-done | bytes 294944 | tf_op jit(solution)/shard_map/ppermute | solution.py:251
  41.3 1.3 gather_fusion.4
  42.6 4.2 %all-to-all-start.1 = ((bf16[4,2,128,128]{3,2,1,0:T(8,128)(2,1)}), bf16[4,2,128,128]{3,2,1,0:T(8,128)(2,1)}, u32[]{:S(2)}, u32[]{:S(2)}) async-start(bf16[4,2,128,128]{3,2,1,0:T(8,128)(2,1)} %bitcast.27), calls=%async_computation.1 | async-start | bytes 524288 | tf_op jit(solution)/shard_map/all_to_all | solution.py:310
  46.8 2.7 %constant_dynamic-slice_fusion = (bf16[128,1024]{1,0:T(8,128)(2,1)S(1)}, bf16[128,1024]{1,0:T(8,128)(2,1)}, bf16[128,1024]{1,0:T(8,128)(2,1)}, bf16[128,1024]{1,...) fusion(bf16[128,8192]{1,0:T(8,128)(2,1)} %bitcast.89, ...), kind=kLoop, calls=%fused_computation.20 | loop fusion | bytes 4194336 | tf_op jit(solution)/shard_map/dynamic_slice | solution.py:291
  49.9 4.8 %collective-permute-start.4 = (bf16[128,1024]{1,0:T(8,128)(2,1)}, bf16[128,1024]{1,0:T(8,128)(2,1)S(1)}, u32[]{:S(2)}, u32[]{:S(2)}) collective-permute-start(bf16[128,1024]{1,0:T(8,128)(2,1)} %get-tuple-element.40), channel_id=1, source_target_pairs={{0,9},{1,8},{8,1},{9,0},{16,25},{17,24},{24,17},{25,16},{2,11},{3,... | collective-permute-start | bytes 786440 | tf_op jit(solution)/shard_map/ppermute | solution.py:255
  54.7 0.9 collective-permute-start.3
  55.6 2.2 %gather_fusion.5 = bf16[4,128,128]{2,1,0:T(8,128)(2,1)} fusion(bf16[8,128,128]{2,1,0:T(8,128)(2,1)} %bitcast.28, s32[1024]{0:T(1024)S(1)} %pad_clamp_fusion), kind=kCustom, calls=%fused_computation.5 | custom fusion | bytes 262160 | tf_op jit(solution)/shard_map/gather | solution.py:314
  59.4 2.9 %collective-permute-start.9 = (bf16[128,1024]{1,0:T(8,128)(2,1)}, bf16[128,1024]{1,0:T(8,128)(2,1)}, u32[]{:S(2)}, u32[]{:S(2)}) collective-permute-start(bf16[128,1024]{1,0:T(8,128)(2,1)} %get-tuple-element.39), channel_id=1, source_target_pairs={{0,17},{1,16},{8,25},{9,24},{16,1},{17,0},{24,9},{25,8},{2,19},{3,... | collective-permute-start | bytes 786440 | tf_op jit(solution)/shard_map/ppermute | solution.py:255
  62.3 5.0 %collective-permute-done.4.refs_1_ = bf16[128,1024]{1,0:T(8,128)(2,1)S(1)} collective-permute-done((bf16[128,1024]{1,0:T(8,128)(2,1)}, bf16[128,1024]{1,0:T(8,128)(2,1)S(1)}, u32[]{:S(2)}, u32[]{:S(2)}) %collective-permute-start.4) | collective-permute-done | bytes 262176 | tf_op jit(solution)/shard_map/ppermute | solution.py:255
  68.2 7.8 %collective-permute-start.13 = (bf16[128,1024]{1,0:T(8,128)(2,1)}, bf16[128,1024]{1,0:T(8,128)(2,1)}, u32[]{:S(2)}, u32[]{:S(2)}) collective-permute-start(bf16[128,1024]{1,0:T(8,128)(2,1)} %get-tuple-element.38), channel_id=1, source_target_pairs={{0,25},{1,24},{8,17},{9,16},{16,9},{17,8},{24,1},{25,0},{2,27},{3,... | collective-permute-start | bytes 786440 | tf_op jit(solution)/shard_map/ppermute | solution.py:255
  76.5 11.6 %shard_map.82 = (f32[152,1024]{1,0:T(8,128)S(1)}, f32[152,1024]{1,0:T(8,128)S(1)}) custom-call(s32[7,2]{1,0:T(8,128)S(1)} %copy.44.plan, bf16[128,1024]{1,0:T(8,128)(2,1)S(1)} %collective-permute-done.2.refs_0_, bf16[128,1024]{1,0:T(8,128)(2,1)S(1)} %collective-permute-done.4.refs_1_, bf16[8,288,128]{2,1,0:T(8,128)(2,1)S(1)} %all-to-all-done.refs_2_, ...), custom_call_target="tpu_custom_call" | custom-call | tf_op jit(solution)/shard_map/pallas_call | solution.py:223
  88.1 1.2 pad_maximum_fusion.1.refs_6_.refs_4_
  89.3 19.3 %shard_map.83 = (bf16[128,1024]{1,0:T(8,128)(2,1)S(1)}, bf16[128,1024]{1,0:T(8,128)(2,1)S(1)}) custom-call(s32[7,2]{1,0:T(8,128)S(1)} %copy.43.plan, bf16[128,1024]{1,0:T(8,128)(2,1)S(1)} %collective-permute-done.3.refs_0_, bf16[128,1024]{1,0:T(8,128)(2,1)} %collective-permute-done.9.refs_1_, bf16[8,288,128]{2,1,0:T(8,128)(2,1)S(1)} %all-to-all-done.refs_2_, ...), custom_call_target="tpu_custom_call" | custom-call | tf_op jit(solution)/shard_map/pallas_call | solution.py:223
  108.6 5.2 %shard_map.84 = (bf16[128,1024]{1,0:T(8,128)(2,1)S(1)}, bf16[128,1024]{1,0:T(8,128)(2,1)S(1)}) custom-call(s32[7,2]{1,0:T(8,128)S(1)} %copy.44.plan, bf16[128,1024]{1,0:T(8,128)(2,1)S(1)} %collective-permute-done.2.refs_0_, bf16[128,1024]{1,0:T(8,128)(2,1)S(1)} %collective-permute-done.4.refs_1_, f32[152,1024]{1,0:T(8,128)S(1)} %get-tuple-element.21.refs_2_, ...), custom_call_target="tpu_custom_call" | custom-call | tf_op jit(solution)/shard_map/pallas_call | solution.py:223
  113.8 19.6 %shard_map.85 = (bf16[128,1024]{1,0:T(8,128)(2,1)S(1)}, bf16[128,1024]{1,0:T(8,128)(2,1)S(1)}) custom-call(s32[7,2]{1,0:T(8,128)S(1)} %copy.45.plan, bf16[128,1024]{1,0:T(8,128)(2,1)} %collective-permute-done.1.refs_0_, bf16[128,1024]{1,0:T(8,128)(2,1)} %collective-permute-done.13.refs_1_, bf16[8,288,128]{2,1,0:T(8,128)(2,1)S(1)} %all-to-all-done.refs_2_, ...), custom_call_target="tpu_custom_call" | custom-call | tf_op jit(solution)/shard_map/pallas_call | solution.py:223
  133.4 10.2 %shard_map.86 = (bf16[128,1024]{1,0:T(8,128)(2,1)S(1)}, bf16[128,1024]{1,0:T(8,128)(2,1)S(1)}) custom-call(s32[7,2]{1,0:T(8,128)S(1)} %copy.46.plan, bf16[128,1024]{1,0:T(8,128)(2,1)} %collective-permute-done.refs_0_, bf16[128,1024]{1,0:T(8,128)(2,1)S(1)} %get-tuple-element.37.refs_1_, bf16[8,288,128]{2,1,0:T(8,128)(2,1)S(1)} %all-to-all-done.refs_2_, ...), custom_call_target="tpu_custom_call" | custom-call | tf_op jit(solution)/shard_map/pallas_call | solution.py:223
  143.9 1.2 collective-permute-start.15
  145.9 1.8 %collective-permute-start.19 = (bf16[128,1024]{1,0:T(8,128)(2,1)S(1)}, bf16[128,1024]{1,0:T(8,128)(2,1)S(1)}, u32[]{:S(2)}, u32[]{:S(2)}) collective-permute-start(bf16[128,1024]{1,0:T(8,128)(2,1)S(1)} %get-tuple-element.28), channel_id=1, source_target_pairs={{0,24},{1,25},{8,16},{9,17},{16,8},{17,9},{24,0},{25,1},{2,26},{3,... | collective-permute-start | bytes 786440 | tf_op jit(solution)/shard_map/ppermute | solution.py:255
  147.8 1.0 collective-permute-start.16
  149.0 1.4 collective-permute-start.18
  150.4 1.1 collective-permute-done.15
  151.5 2.6 %collective-permute-start.20 = (bf16[128,1024]{1,0:T(8,128)(2,1)S(1)}, bf16[128,1024]{1,0:T(8,128)(2,1)S(1)}, u32[]{:S(2)}, u32[]{:S(2)}) collective-permute-start(bf16[128,1024]{1,0:T(8,128)(2,1)S(1)} %get-tuple-element.34), channel_id=1, source_target_pairs={{0,25},{1,24},{8,17},{9,16},{16,9},{17,8},{24,1},{25,0},{2,27},{3,... | collective-permute-start | bytes 786440 | tf_op jit(solution)/shard_map/ppermute | solution.py:255
  154.1 10.1 %collective-permute-done.16 = bf16[128,1024]{1,0:T(8,128)(2,1)S(1)} collective-permute-done((bf16[128,1024]{1,0:T(8,128)(2,1)S(1)}, bf16[128,1024]{1,0:T(8,128)(2,1)S(1)}, u32[]{:S(2)}, u32[]{:S(2)}) %collective-permute-start.16) | collective-permute-done | bytes 262176 | tf_op jit(solution)/shard_map/ppermute | solution.py:255
  164.3 5.2 %collective-permute-done.18 = bf16[128,1024]{1,0:T(8,128)(2,1)S(1)} collective-permute-done((bf16[128,1024]{1,0:T(8,128)(2,1)S(1)}, bf16[128,1024]{1,0:T(8,128)(2,1)S(1)}, u32[]{:S(2)}, u32[]{:S(2)}) %collective-permute-start.18) | collective-permute-done | bytes 262176 | tf_op jit(solution)/shard_map/ppermute | solution.py:255
  169.6 2.5 %collective-permute-done.20 = bf16[128,1024]{1,0:T(8,128)(2,1)S(1)} collective-permute-done((bf16[128,1024]{1,0:T(8,128)(2,1)S(1)}, bf16[128,1024]{1,0:T(8,128)(2,1)S(1)}, u32[]{:S(2)}, u32[]{:S(2)}) %collective-permute-start.20) | collective-permute-done | bytes 262176 | tf_op jit(solution)/shard_map/ppermute | solution.py:255
  (85 shorter events, 8.9 us)
Async XLA Ops:
  0.0 19.6 %copy-start = (s32[4,16,4]{1,2,0:T(4,128)S(1)}, s32[4,16,4]{1,2,0:T(4,128)}, u32[]{:S(2)}) copy-start(s32[4,16,4]{1,2,0:T(4,128)} %param.15) | copy-start | bytes 3076
  0.0 8.0 %copy-start.2 = (s32[4,4]{1,0:T(4,128)S(1)}, s32[4,4]{1,0:T(4,128)}, u32[]{:S(2)}) copy-start(s32[4,4]{1,0:T(4,128)} %param.13) | copy-start | bytes 196
  0.0 8.3 %copy-start.3 = (s32[4,4]{1,0:T(4,128)S(1)}, s32[4,4]{1,0:T(4,128)}, u32[]{:S(2)}) copy-start(s32[4,4]{1,0:T(4,128)} %param.14) | copy-start | bytes 196
  2.0 16.0 %all-to-all-start = ((bf16[8,288,128]{2,1,0:T(8,128)(2,1)}), bf16[8,288,128]{2,1,0:T(8,128)(2,1)S(1)}, u32[]{:S(2)}, u32[]{:S(2)}) async-start(bf16[8,288,128]{2,1,0:T(8,128)(2,1)} %packing.1), calls=%async_computation | async-start | bytes 1179648 | tf_op jit(solution)/shard_map/all_to_all | solution.py:282
  18.1 13.9 %collective-permute-start.5 = (bf16[8,288,128]{2,1,0:T(8,128)(2,1)S(1)}, bf16[8,288,128]{2,1,0:T(8,128)(2,1)S(1)}, u32[]{:S(2)}, u32[]{:S(2)}) collective-permute-start(bf16[8,288,128]{2,1,0:T(8,128)(2,1)S(1)} %all-to-all-done.refs_2_), channel_id=1, source_target_pairs={{0,2},{2,4},{4,6},{6,0},{1,3},{3,5},{5,7},{7,1},{8,10},{10,12},{12... | collective-permute-start | bytes 1769480 | tf_op jit(solution)/shard_map/ppermute | solution.py:251
  18.1 15.3 %collective-permute-start.7 = (bf16[8,288,128]{2,1,0:T(8,128)(2,1)S(1)}, bf16[8,288,128]{2,1,0:T(8,128)(2,1)S(1)}, u32[]{:S(2)}, u32[]{:S(2)}) collective-permute-start(bf16[8,288,128]{2,1,0:T(8,128)(2,1)S(1)} %all-to-all-done.refs_2_), channel_id=1, source_target_pairs={{0,6},{2,0},{4,2},{6,4},{1,7},{3,1},{5,3},{7,5},{8,14},{10,8},{12,... | collective-permute-start | bytes 1769480 | tf_op jit(solution)/shard_map/ppermute | solution.py:251
  32.0 6.8 %collective-permute-start.6 = (bf16[4,288,128]{2,1,0:T(8,128)(2,1)S(1)}, bf16[4,288,128]{2,1,0:T(8,128)(2,1)S(1)}, u32[]{:S(2)}, u32[]{:S(2)}) collective-permute-start(bf16[4,288,128]{2,1,0:T(8,128)(2,1)S(1)} %slice.20), channel_id=1, source_target_pairs={{0,2},{2,4},{4,6},{6,0},{1,3},{3,5},{5,7},{7,1},{8,10},{10,12},{12... | collective-permute-start | bytes 884744 | tf_op jit(solution)/shard_map/ppermute | solution.py:251
  33.4 7.8 %collective-permute-start.8 = (bf16[4,288,128]{2,1,0:T(8,128)(2,1)S(1)}, bf16[4,288,128]{2,1,0:T(8,128)(2,1)S(1)}, u32[]{:S(2)}, u32[]{:S(2)}) collective-permute-start(bf16[4,288,128]{2,1,0:T(8,128)(2,1)S(1)} %slice.21), channel_id=1, source_target_pairs={{0,6},{2,0},{4,2},{6,4},{1,7},{3,1},{5,3},{7,5},{8,14},{10,8},{12,... | collective-permute-start | bytes 884744 | tf_op jit(solution)/shard_map/ppermute | solution.py:251
  42.6 12.9 %all-to-all-start.1 = ((bf16[4,2,128,128]{3,2,1,0:T(8,128)(2,1)}), bf16[4,2,128,128]{3,2,1,0:T(8,128)(2,1)}, u32[]{:S(2)}, u32[]{:S(2)}) async-start(bf16[4,2,128,128]{3,2,1,0:T(8,128)(2,1)} %bitcast.27), calls=%async_computation.1 | async-start | bytes 524288 | tf_op jit(solution)/shard_map/all_to_all | solution.py:310
  49.6 9.8 %collective-permute-start.2 = (bf16[128,1024]{1,0:T(8,128)(2,1)}, bf16[128,1024]{1,0:T(8,128)(2,1)S(1)}, u32[]{:S(2)}, u32[]{:S(2)}) collective-permute-start(bf16[128,1024]{1,0:T(8,128)(2,1)} %get-tuple-element.42), channel_id=1, source_target_pairs={{0,8},{1,9},{8,0},{9,1},{16,24},{17,25},{24,16},{25,17},{2,10},{3,... | collective-permute-start | bytes 786440 | tf_op jit(solution)/shard_map/ppermute | solution.py:255
  49.9 17.5 %collective-permute-start.4 = (bf16[128,1024]{1,0:T(8,128)(2,1)}, bf16[128,1024]{1,0:T(8,128)(2,1)S(1)}, u32[]{:S(2)}, u32[]{:S(2)}) collective-permute-start(bf16[128,1024]{1,0:T(8,128)(2,1)} %get-tuple-element.40), channel_id=1, source_target_pairs={{0,9},{1,8},{8,1},{9,0},{16,25},{17,24},{24,17},{25,16},{2,11},{3,... | collective-permute-start | bytes 786440 | tf_op jit(solution)/shard_map/ppermute | solution.py:255
  54.7 13.6 %collective-permute-start.3 = (bf16[128,1024]{1,0:T(8,128)(2,1)}, bf16[128,1024]{1,0:T(8,128)(2,1)S(1)}, u32[]{:S(2)}, u32[]{:S(2)}) collective-permute-start(bf16[128,1024]{1,0:T(8,128)(2,1)} %get-tuple-element.41), channel_id=1, source_target_pairs={{0,16},{1,17},{8,24},{9,25},{16,0},{17,1},{24,8},{25,9},{2,18},{3,... | collective-permute-start | bytes 786440 | tf_op jit(solution)/shard_map/ppermute | solution.py:255
  57.7 18.3 %collective-permute-start.10 = (bf16[4,128,128]{2,1,0:T(8,128)(2,1)}, bf16[4,128,128]{2,1,0:T(8,128)(2,1)}, u32[]{:S(2)}, u32[]{:S(2)}) collective-permute-start(bf16[4,128,128]{2,1,0:T(8,128)(2,1)} %gather_fusion.5), channel_id=1, source_target_pairs={{0,2},{2,4},{4,6},{6,0},{1,3},{3,5},{5,7},{7,1},{8,10},{10,12},{12... | collective-permute-start | bytes 393224 | tf_op jit(solution)/shard_map/ppermute | solution.py:251
  57.7 18.3 %collective-permute-start.11 = (bf16[4,128,128]{2,1,0:T(8,128)(2,1)}, bf16[4,128,128]{2,1,0:T(8,128)(2,1)}, u32[]{:S(2)}, u32[]{:S(2)}) collective-permute-start(bf16[4,128,128]{2,1,0:T(8,128)(2,1)} %gather_fusion.5), channel_id=1, source_target_pairs={{0,4},{2,6},{4,0},{6,2},{1,5},{3,7},{5,1},{7,3},{8,12},{10,14},{12... | collective-permute-start | bytes 393224 | tf_op jit(solution)/shard_map/ppermute | solution.py:251
  59.4 29.9 %collective-permute-start.9 = (bf16[128,1024]{1,0:T(8,128)(2,1)}, bf16[128,1024]{1,0:T(8,128)(2,1)}, u32[]{:S(2)}, u32[]{:S(2)}) collective-permute-start(bf16[128,1024]{1,0:T(8,128)(2,1)} %get-tuple-element.39), channel_id=1, source_target_pairs={{0,17},{1,16},{8,25},{9,24},{16,1},{17,0},{24,9},{25,8},{2,19},{3,... | collective-permute-start | bytes 786440 | tf_op jit(solution)/shard_map/ppermute | solution.py:255
  67.4 46.4 %collective-permute-start.1 = (bf16[128,1024]{1,0:T(8,128)(2,1)}, bf16[128,1024]{1,0:T(8,128)(2,1)}, u32[]{:S(2)}, u32[]{:S(2)}) collective-permute-start(bf16[128,1024]{1,0:T(8,128)(2,1)} %get-tuple-element.43), channel_id=1, source_target_pairs={{0,24},{1,25},{8,16},{9,17},{16,8},{17,9},{24,0},{25,1},{2,26},{3,... | collective-permute-start | bytes 786440 | tf_op jit(solution)/shard_map/ppermute | solution.py:255
  68.2 45.6 %collective-permute-start.13 = (bf16[128,1024]{1,0:T(8,128)(2,1)}, bf16[128,1024]{1,0:T(8,128)(2,1)}, u32[]{:S(2)}, u32[]{:S(2)}) collective-permute-start(bf16[128,1024]{1,0:T(8,128)(2,1)} %get-tuple-element.38), channel_id=1, source_target_pairs={{0,25},{1,24},{8,17},{9,16},{16,9},{17,8},{24,1},{25,0},{2,27},{3,... | collective-permute-start | bytes 786440 | tf_op jit(solution)/shard_map/ppermute | solution.py:255
  76.0 57.4 %collective-permute-start = (bf16[128,1024]{1,0:T(8,128)(2,1)}, bf16[128,1024]{1,0:T(8,128)(2,1)}, u32[]{:S(2)}, u32[]{:S(2)}) collective-permute-start(bf16[128,1024]{1,0:T(8,128)(2,1)} %get-tuple-element.44), channel_id=1, source_target_pairs={{0,1},{1,0},{8,9},{9,8},{16,17},{17,16},{24,25},{25,24},{2,3},{3,2... | collective-permute-start | bytes 786440 | tf_op jit(solution)/shard_map/ppermute | solution.py:255
  76.0 12.0 %collective-permute-start.12 = (bf16[4,128,128]{2,1,0:T(8,128)(2,1)}, bf16[4,128,128]{2,1,0:T(8,128)(2,1)}, u32[]{:S(2)}, u32[]{:S(2)}) collective-permute-start(bf16[4,128,128]{2,1,0:T(8,128)(2,1)} %gather_fusion.5), channel_id=1, source_target_pairs={{0,6},{2,0},{4,2},{6,4},{1,7},{3,1},{5,3},{7,5},{8,14},{10,8},{12,... | collective-permute-start | bytes 393224 | tf_op jit(solution)/shard_map/ppermute | solution.py:251
  143.6 5.4 %collective-permute-start.14 = (bf16[128,1024]{1,0:T(8,128)(2,1)S(1)}, bf16[128,1024]{1,0:T(8,128)(2,1)S(1)}, u32[]{:S(2)}, u32[]{:S(2)}) collective-permute-start(bf16[128,1024]{1,0:T(8,128)(2,1)S(1)} %get-tuple-element.31), channel_id=1, source_target_pairs={{0,1},{1,0},{8,9},{9,8},{16,17},{17,16},{24,25},{25,24},{2,3},{3,2... | collective-permute-start | bytes 786440 | tf_op jit(solution)/shard_map/ppermute | solution.py:255
  143.9 7.6 %collective-permute-start.15 = (bf16[128,1024]{1,0:T(8,128)(2,1)S(1)}, bf16[128,1024]{1,0:T(8,128)(2,1)S(1)}, u32[]{:S(2)}, u32[]{:S(2)}) collective-permute-start(bf16[128,1024]{1,0:T(8,128)(2,1)S(1)} %get-tuple-element.26), channel_id=1, source_target_pairs={{0,8},{1,9},{8,0},{9,1},{16,24},{17,25},{24,16},{25,17},{2,10},{3,... | collective-permute-start | bytes 786440 | tf_op jit(solution)/shard_map/ppermute | solution.py:255
  145.1 19.2 %collective-permute-start.17 = (bf16[128,1024]{1,0:T(8,128)(2,1)S(1)}, bf16[128,1024]{1,0:T(8,128)(2,1)S(1)}, u32[]{:S(2)}, u32[]{:S(2)}) collective-permute-start(bf16[128,1024]{1,0:T(8,128)(2,1)S(1)} %get-tuple-element.23), channel_id=1, source_target_pairs={{0,16},{1,17},{8,24},{9,25},{16,0},{17,1},{24,8},{25,9},{2,18},{3,... | collective-permute-start | bytes 786440 | tf_op jit(solution)/shard_map/ppermute | solution.py:255
  145.9 23.6 %collective-permute-start.19 = (bf16[128,1024]{1,0:T(8,128)(2,1)S(1)}, bf16[128,1024]{1,0:T(8,128)(2,1)S(1)}, u32[]{:S(2)}, u32[]{:S(2)}) collective-permute-start(bf16[128,1024]{1,0:T(8,128)(2,1)S(1)} %get-tuple-element.28), channel_id=1, source_target_pairs={{0,24},{1,25},{8,16},{9,17},{16,8},{17,9},{24,0},{25,1},{2,26},{3,... | collective-permute-start | bytes 786440 | tf_op jit(solution)/shard_map/ppermute | solution.py:255
  147.8 16.5 %collective-permute-start.16 = (bf16[128,1024]{1,0:T(8,128)(2,1)S(1)}, bf16[128,1024]{1,0:T(8,128)(2,1)S(1)}, u32[]{:S(2)}, u32[]{:S(2)}) collective-permute-start(bf16[128,1024]{1,0:T(8,128)(2,1)S(1)} %get-tuple-element.32), channel_id=1, source_target_pairs={{0,9},{1,8},{8,1},{9,0},{16,25},{17,24},{24,17},{25,16},{2,11},{3,... | collective-permute-start | bytes 786440 | tf_op jit(solution)/shard_map/ppermute | solution.py:255
  149.0 20.5 %collective-permute-start.18 = (bf16[128,1024]{1,0:T(8,128)(2,1)S(1)}, bf16[128,1024]{1,0:T(8,128)(2,1)S(1)}, u32[]{:S(2)}, u32[]{:S(2)}) collective-permute-start(bf16[128,1024]{1,0:T(8,128)(2,1)S(1)} %get-tuple-element.33), channel_id=1, source_target_pairs={{0,17},{1,16},{8,25},{9,24},{16,1},{17,0},{24,9},{25,8},{2,19},{3,... | collective-permute-start | bytes 786440 | tf_op jit(solution)/shard_map/ppermute | solution.py:255
  151.5 20.5 %collective-permute-start.20 = (bf16[128,1024]{1,0:T(8,128)(2,1)S(1)}, bf16[128,1024]{1,0:T(8,128)(2,1)S(1)}, u32[]{:S(2)}, u32[]{:S(2)}) collective-permute-start(bf16[128,1024]{1,0:T(8,128)(2,1)S(1)} %get-tuple-element.34), channel_id=1, source_target_pairs={{0,25},{1,24},{8,17},{9,16},{16,9},{17,8},{24,1},{25,0},{2,27},{3,... | collective-permute-start | bytes 786440 | tf_op jit(solution)/shard_map/ppermute | solution.py:255
  169.6 2.5 %copy-start.1 = (bf16[1,128,8192]{2,1,0:T(8,128)(2,1)}, bf16[1,128,8192]{2,1,0:T(8,128)(2,1)S(1)}, u32[]{:S(2)}) copy-start(bf16[1,128,8192]{2,1,0:T(8,128)(2,1)S(1)} %bitcast_dynamic-update-slice_fusion.1) | copy-start | bytes 6291460
where the time goes:
time: 173 us
  Pallas kernels  67.8 us (39%)
  waiting for transfers between devices  50.8 us (29%)
  starting transfers between devices  41.1 us (24%)
  local copies, waits for them, and re-layouts  10.4 us (6%)
  other arithmetic  2.21 us (1%)
    pallas_call x5, Pallas kernels, attend(): pl.pallas_call(make_kernel(kind, chunks), out_shape=(result,) * chunks, g...  65.8 us
    ppermute x14, starting transfers between devices, exchanged(): return lax.ppermute(value, (Z, CORE), [(k, k ^ step) for k in range(8)])  26.8 us
    ppermute x14, waiting for transfers between devices, exchanged(): return lax.ppermute(value, (Z, CORE), [(k, k ^ step) for k in range(8)])  23.9 us
    ppermute x7, waiting for transfers between devices, shifted(): return lax.ppermute(value, axis, [(k, (k + by) % n) for k in range(n)])  17.9 us
    all_to_all x1, waiting for transfers between devices, attention(): lax.all_to_all(send, (Z, CORE), split_axis=0, concat_axis=0, tiled=True)  9.02 us
    all_to_all x1, starting transfers between devices, attention(): lax.all_to_all(send, (Z, CORE), split_axis=0, concat_axis=0, tiled=True)  5.98 us
    all_to_all x1, starting transfers between devices, attention(): lax.all_to_all(mine[place], 'branch', split_axis=0, concat_axis=0, tiled=...  4.21 us
    ppermute x7, starting transfers between devices, shifted(): return lax.ppermute(value, axis, [(k, (k + by) % n) for k in range(n)])  4.16 us
  transfers between devices with their start and end apart: 23, of which 9 were waited for; matrix products, arithmetic and copies ran while one was open for 6% of the time, Pallas kernels for 32%

commit v1 on v0

--- a/solution.py
+++ b/solution.py
@@ -55,10 +55,11 @@
                 pairs.append((own.at[:, pl.ds(0, TOK)], kbuf.at[here]))
                 pairs.append((own.at[:, pl.ds(TOK, HD)], vbuf.at[here, pl.ds(0, HD)]))
                 pairs.append((own.at[:, pl.ds(TOK + HD, 2 * PAST)], past.at[r]))
-            for t in range(4 if has_sib else 0):
-                source = sibs[0].at[lax.rem(y + 4 - t, 4)]
-                here = pl.ds(SIB0 + 4 * (t % 2), 4)
-                pairs.append((source, kbuf.at[here] if t < 2 else vbuf.at[here, pl.ds(0, HD)]))
+            for slot in range(NSIB if has_sib else 0):
+                source = sibs[0].at[plan[3 + NSIB + slot, 0]]
+                here = pl.ds(SIB0 + 2 * slot, 2)
+                pairs.append((source.at[:, pl.ds(0, TOK)], kbuf.at[here]))
+                pairs.append((source.at[:, pl.ds(TOK, HD)], vbuf.at[here, pl.ds(0, HD)]))
             copies = [pltpu.make_async_copy(a, b, sem.at[i]) for i, (a, b) in enumerate(pairs)]
             for copy in copies:
                 copy.start()
@@ -111,8 +112,8 @@
                 n = n + jnp.where(y >= r, 2, 0)
         if has_sib:
             for slot in range(NSIB):
-                todo[n] = SIB0 + slot
-                todo[n + 1] = SIB0 + 4 + slot
+                todo[n] = SIB0 + 2 * slot
+                todo[n + 1] = SIB0 + 2 * slot + 1
                 n = n + jnp.where(plan[3 + slot, step] == 1, 2, 0)
         repeat = todo[1 if has_own else 0]
         for t in range(2 * SPAN):
@@ -239,7 +240,7 @@
                 pltpu.VMEM((1, GROUP), jnp.float32),
                 pltpu.VMEM((VROWS, GROUP), jnp.float32),
                 pltpu.VMEM((1, GROUP), jnp.float32),
-                pltpu.SemaphoreType.DMA((16,)),
+                pltpu.SemaphoreType.DMA((20,)),
             ],
         ),
         compiler_params=pltpu.CompilerParams(vmem_limit_bytes=32 * 2**20),
@@ -273,6 +274,41 @@
     return pl.pallas_call(packing, out_shape=shape, name="packing")(*arrays)
 
 
+def picking(where, own0, own1, own2, own3, out_ref, sem):
+    count = out_ref.shape[0]
+
+    def copy(own, e):
+        pair = own.at[pl.ds(2 * where[count + e], 2), pl.ds(0, TOK + HD)]
+        return pltpu.make_async_copy(pair, out_ref.at[e], sem.at[e])
+
+    for e in range(count):
+        for r, own in enumerate((own0, own1, own2, own3)):
+
+            @pl.when(where[e] == r)
+            def _(own=own, e=e):
+                copy(own, e).start()
+
+    for e in range(count):
+        copy(own0, e).wait()
+
+
+def picked(where, owns):
+    entries = where.shape[0] // 2
+    raw = pl.BlockSpec(memory_space=pl.ANY)
+    return pl.pallas_call(
+        picking,
+        out_shape=jax.ShapeDtypeStruct((entries, 2, TOK + HD, HD), jnp.bfloat16),
+        grid_spec=pltpu.PrefetchScalarGridSpec(
+            num_scalar_prefetch=1,
+            grid=(1,),
+            in_specs=[raw] * 4,
+            out_specs=raw,
+            scratch_shapes=[pltpu.SemaphoreType.DMA((entries,))],
+        ),
+        name="picking",
+    )(where, *owns)
+
+
 def attention(query, key_new, value_new, hist_key, hist_value, sib_source, sib_block, sib_mask):
     z, y, core = lax.axis_index(Z), lax.axis_index(Y), lax.axis_index(CORE)
     me = z * 2 + core
@@ -291,13 +327,6 @@
         piece = lax.dynamic_slice_in_dim(cols, (me ^ s) * GROUP, GROUP, 1)
         queries[s] = exchanged(piece, s) if s else piece
 
-    start = TOK * (y // 2)
-    mine = jnp.concatenate(
-        [
-            lax.dynamic_slice(o.reshape(4, 2, -1, HD), (0, y % 2, start, 0), (4, 1, TOK, HD)).reshape(4, TOK, HD)
-            for o in owns
-        ]
-    )
     my_source = lax.dynamic_index_in_dim(sib_source, reader, 0, keepdims=False)
     my_mask = lax.dynamic_index_in_dim(sib_mask, reader, 0, keepdims=False)
     from_me = sib_source == reader
@@ -305,19 +334,20 @@
     slot_hit = from_me[:, :, None] & (
         sender_rank[:, :, None] == jnp.arange(SRCMAX, dtype=jnp.int32)[None, None, :]
     )
-    send_table = jnp.sum(jnp.where(slot_hit, sib_block[:, :, None], 0), axis=1)
-    place = ((y - send_table) % 4) * 4 + send_table // 4
-    got = lax.all_to_all(mine[place], "branch", split_axis=0, concat_axis=0, tiled=True)
+    send_table = jnp.sum(jnp.where(slot_hit, sib_block[:, :, None], 0), axis=1).reshape(-1)
+    where = jnp.concatenate([(y - send_table) % 4, send_table // 4]).astype(jnp.int32)
+    sent = picked(where, owns)
+    sib = lax.all_to_all(sent, "branch", split_axis=0, concat_axis=0, tiled=True)
     slots = jnp.arange(NSIB, dtype=jnp.int32)
     same = (my_source[None, :] == my_source[:, None]) & (slots[None, :] < slots[:, None])
     rank = jnp.sum(same.astype(jnp.int32), axis=1)
-    listed = got.reshape(-1, HD, HD)[my_source * SRCMAX + rank]
-    sib = jnp.stack([listed, shifted(listed, Y, 1), shifted(listed, Y, 2), shifted(listed, Y, -1)])
+    flat = (my_source * SRCMAX + rank).astype(jnp.int32)
 
     def plan_of(steps):
         chunks = jnp.stack([me ^ s for s in steps])
         visible = my_mask[(chunks // 2) * 4 + y]
         rows = [(chunks // 2)[None], (chunks % 2)[None], jnp.broadcast_to(y, (1, len(steps))), visible.T]
+        rows.append(jnp.broadcast_to(flat[:, None], (NSIB, len(steps))))
         return jnp.concatenate(rows, axis=0).astype(jnp.int32)
 
     parts, states, previous = {}, {}, None
@@ -338,8 +368,8 @@
     return out[None]
 
 
-QORDER = (2, 3, 4, 5, 6, 7, 1, 0)
-CALLS = (("open", (2, 3)), ("full", (4, 5)), ("close", (2, 3)), ("full", (6, 7)), ("full", (1, 0)))
+QORDER = (2, 4, 3, 5, 6, 7, 1, 0)
+CALLS = (("open", (2, 4)), ("full", (3, 5)), ("close", (2, 4)), ("full", (6, 0)), ("full", (7, 1)))
 
 
 def solution(mesh):

time: 173 us -> 207 us (1.20)
  the two profiles are of different devices: /device:TPU:31 before, /device:TPU:30 now
where the time goes in v1:
time: 207 us
  Pallas kernels  102 us (49%)
  waiting for transfers between devices  59.5 us (29%)
  starting transfers between devices  30.6 us (15%)
  local copies, waits for them, and re-layouts  13.2 us (6%)
    pallas_call x5, Pallas kernels, attend(): pl.pallas_call(make_kernel(kind, chunks), out_shape=(result,) * chunks, g...  66.1 us
    pallas_call x1, Pallas kernels, picked(): pl.pallas_call(picking, out_shape=jax.ShapeDtypeStruct((entries, 2, TOK +...  33.6 us
    ppermute x14, waiting for transfers between devices, exchanged(): return lax.ppermute(value, (Z, CORE), [(k, k ^ step) for k in range(8)])  29.4 us
    ppermute x4, waiting for transfers between devices, shifted(): return lax.ppermute(value, axis, [(k, (k + by) % n) for k in range(n)])  19.6 us
    ppermute x14, starting transfers between devices, exchanged(): return lax.ppermute(value, (Z, CORE), [(k, k ^ step) for k in range(8)])  16.2 us
    all_to_all x1, waiting for transfers between devices, attention(): lax.all_to_all(send, (Z, CORE), split_axis=0, concat_axis=0, tiled=True)  10.5 us
    unnamed x47, local copies, waits for them, and re-layouts  5.9 us
    all_to_all x1, starting transfers between devices, attention(): lax.all_to_all(send, (Z, CORE), split_axis=0, concat_axis=0, tiled=True)  5.31 us
  transfers between devices with their start and end apart: 20, of which 11 were waited for; matrix products, arithmetic and copies ran while one was open for 4% of the time, Pallas kernels for 25%

profile of v1, /device:TPU:30, one launch (start us, length us, event | category | flops | bytes accessed | tf_op | source)
XLA Modules:
  0.0 206.8 jit_solution(14587305683099873157)
XLA Ops:
  0.0 2.0 packing.1
  2.0 5.3 %all-to-all-start = ((bf16[8,288,128]{2,1,0:T(8,128)(2,1)}), bf16[8,288,128]{2,1,0:T(8,128)(2,1)S(1)}, u32[]{:S(2)}, u32[]{:S(2)}) async-start(bf16[8,288,128]{2,1,0:T(8,128)(2,1)} %packing.1), calls=%async_computation | async-start | bytes 1179648 | tf_op jit(solution)/shard_map/all_to_all | solution.py:318
  7.8 10.5 %all-to-all-done.refs_2_.own0 = bf16[8,288,128]{2,1,0:T(8,128)(2,1)S(1)} async-done(((bf16[8,288,128]{2,1,0:T(8,128)(2,1)}), bf16[8,288,128]{2,1,0:T(8,128)(2,1)S(1)}, u32[]{:S(2)}, u32[]{:S(2)}) %all-to-all-start) | async-done | bytes 589856 | tf_op jit(solution)/shard_map/all_to_all | solution.py:318
  18.6 1.9 collective-permute-start.6
  20.8 12.3 %collective-permute-done.4.refs_3_.own1 = bf16[8,288,128]{2,1,0:T(8,128)(2,1)S(1)} collective-permute-done((bf16[8,288,128]{2,1,0:T(8,128)(2,1)S(1)}, bf16[8,288,128]{2,1,0:T(8,128)(2,1)S(1)}, u32[]{:S(2)}, u32[]{:S(2)}) %collective-permute-start.4) | collective-permute-done | bytes 589856 | tf_op jit(solution)/shard_map/ppermute | solution.py:252
  33.2 1.6 collective-permute-start.5
  36.1 4.7 %collective-permute-done.5 = bf16[4,288,128]{2,1,0:T(8,128)(2,1)S(1)} collective-permute-done((bf16[4,288,128]{2,1,0:T(8,128)(2,1)S(1)}, bf16[4,288,128]{2,1,0:T(8,128)(2,1)S(1)}, u32[]{:S(2)}, u32[]{:S(2)}) %collective-permute-start.5) | collective-permute-done | bytes 294944 | tf_op jit(solution)/shard_map/ppermute | solution.py:252
  40.8 2.6 %collective-permute-done.7 = bf16[4,288,128]{2,1,0:T(8,128)(2,1)S(1)} collective-permute-done((bf16[4,288,128]{2,1,0:T(8,128)(2,1)S(1)}, bf16[4,288,128]{2,1,0:T(8,128)(2,1)S(1)}, u32[]{:S(2)}, u32[]{:S(2)}) %collective-permute-start.7) | collective-permute-done | bytes 294944 | tf_op jit(solution)/shard_map/ppermute | solution.py:252
  44.3 33.6 %picking.1 = bf16[8,2,256,128]{3,2,1,0:T(8,128)(2,1)} custom-call(s32[16]{0:T(128)} %pad_add_fusion.7.where, bf16[8,288,128]{2,1,0:T(8,128)(2,1)} %copy-done.1, bf16[8,288,128]{2,1,0:T(8,128)(2,1)} %copy-done.3, bf16[8,288,128]{2,1,0:T(8,128)(2,1)} %copy-done.7, bf16[8,288,128]{2,1,0:T(8,128)(2,1)} %copy-done.5), custom_call_target="tpu_custom_call" | custom-call | tf_op jit(solution)/shard_map/picking/pallas_call | solution.py:298
  78.0 4.8 %all-to-all-start.1 = ((bf16[8,2,256,128]{3,2,1,0:T(8,128)(2,1)}), bf16[8,2,256,128]{3,2,1,0:T(8,128)(2,1)S(1)}, u32[]{:S(2)}, u32[]{:S(2)}) async-start(bf16[8,2,256,128]{3,2,1,0:T(8,128)(2,1)} %picking.1), calls=%async_computation.1 | async-start | bytes 2097152 | tf_op jit(solution)/shard_map/all_to_all | solution.py:340
  82.7 2.9 %constant_dynamic-slice_fusion = (bf16[128,1024]{1,0:T(8,128)(2,1)}, bf16[128,1024]{1,0:T(8,128)(2,1)}, bf16[128,1024]{1,0:T(8,128)(2,1)}, bf16[128,1024]{1,0:T(...) fusion(bf16[128,8192]{1,0:T(8,128)(2,1)} %bitcast.43, ...), kind=kLoop, calls=%fused_computation.12 | loop fusion | bytes 4194336 | tf_op jit(solution)/shard_map/dynamic_slice | solution.py:327
  86.2 2.1 collective-permute-start.3
  88.4 3.2 %collective-permute-start.8 = (bf16[128,1024]{1,0:T(8,128)(2,1)}, bf16[128,1024]{1,0:T(8,128)(2,1)}, u32[]{:S(2)}, u32[]{:S(2)}) collective-permute-start(bf16[128,1024]{1,0:T(8,128)(2,1)} %get-tuple-element.40), channel_id=1, source_target_pairs={{0,17},{1,16},{8,25},{9,24},{16,1},{17,0},{24,9},{25,8},{2,19},{3,... | collective-permute-start | bytes 786440 | tf_op jit(solution)/shard_map/ppermute | solution.py:256
  91.6 1.2 collective-permute-start
  92.8 2.0 collective-permute-done.1.refs_0_
  95.5 5.6 %collective-permute-done.3.refs_1_ = bf16[128,1024]{1,0:T(8,128)(2,1)S(1)} collective-permute-done((bf16[128,1024]{1,0:T(8,128)(2,1)S(1)}, bf16[128,1024]{1,0:T(8,128)(2,1)S(1)}, u32[]{:S(2)}, u32[]{:S(2)}) %collective-permute-start.3) | collective-permute-done | bytes 262176 | tf_op jit(solution)/shard_map/ppermute | solution.py:256
  105.0 0.9 copy-done.11
  106.0 0.9 copy-done.14
  106.9 13.2 %shard_map.82 = (f32[152,1024]{1,0:T(8,128)S(1)}, f32[152,1024]{1,0:T(8,128)S(1)}) custom-call(s32[11,2]{1,0:T(8,128)S(1)} %copy.40.plan, bf16[128,1024]{1,0:T(8,128)(2,1)S(1)} %copy-done.11, bf16[128,1024]{1,0:T(8,128)(2,1)S(1)} %copy-done.14, bf16[8,288,128]{2,1,0:T(8,128)(2,1)S(1)} %copy-done.2, bf16[8,288,128]{2,1,0:T(8,128)(2,1)S(1)} %copy-done.4, ...), custom_call_target="tpu_custom_call" | custom-call | tf_op jit(solution)/shard_map/pallas_call | solution.py:224
  121.9 17.8 %shard_map.83 = (bf16[128,1024]{1,0:T(8,128)(2,1)S(1)}, bf16[128,1024]{1,0:T(8,128)(2,1)S(1)}) custom-call(s32[11,2]{1,0:T(8,128)S(1)} %copy.39.plan, bf16[128,1024]{1,0:T(8,128)(2,1)} %collective-permute-done.2.refs_0_, bf16[128,1024]{1,0:T(8,128)(2,1)} %collective-permute-done.8.refs_1_, bf16[8,288,128]{2,1,0:T(8,128)(2,1)S(1)} %copy-done.2, ...), custom_call_target="tpu_custom_call" | custom-call | tf_op jit(solution)/shard_map/pallas_call | solution.py:224
  139.8 5.3 %shard_map.84 = (bf16[128,1024]{1,0:T(8,128)(2,1)S(1)}, bf16[128,1024]{1,0:T(8,128)(2,1)S(1)}) custom-call(s32[11,2]{1,0:T(8,128)S(1)} %copy.40.plan, bf16[128,1024]{1,0:T(8,128)(2,1)S(1)} %copy-done.12, bf16[128,1024]{1,0:T(8,128)(2,1)S(1)} %copy-done.15, f32[152,1024]{1,0:T(8,128)S(1)} %copy-done.17, f32[152,1024]{1,0:T(8,128)S(1)} %copy-done.19, ...), custom_call_target="tpu_custom_call" | custom-call | tf_op jit(solution)/shard_map/pallas_call | solution.py:224
  145.0 15.0 %shard_map.85 = (bf16[128,1024]{1,0:T(8,128)(2,1)S(1)}, bf16[128,1024]{1,0:T(8,128)(2,1)S(1)}) custom-call(s32[11,2]{1,0:T(8,128)S(1)} %copy.41.plan, bf16[128,1024]{1,0:T(8,128)(2,1)} %collective-permute-done.refs_0_, bf16[128,1024]{1,0:T(8,128)(2,1)S(1)} %copy-done.9, bf16[8,288,128]{2,1,0:T(8,128)(2,1)S(1)} %copy-done.2, ...), custom_call_target="tpu_custom_call" | custom-call | tf_op jit(solution)/shard_map/pallas_call | solution.py:224
  160.1 14.8 %shard_map.86 = (bf16[128,1024]{1,0:T(8,128)(2,1)S(1)}, bf16[128,1024]{1,0:T(8,128)(2,1)S(1)}) custom-call(s32[11,2]{1,0:T(8,128)S(1)} %copy.43.plan, bf16[128,1024]{1,0:T(8,128)(2,1)} %collective-permute-done.9.refs_0_, bf16[128,1024]{1,0:T(8,128)(2,1)} %collective-permute-done.10.refs_1_, bf16[8,288,128]{2,1,0:T(8,128)(2,1)S(1)} %copy-done.2, ...), custom_call_target="tpu_custom_call" | custom-call | tf_op jit(solution)/shard_map/pallas_call | solution.py:224
  175.5 3.0 %collective-permute-start.12 = (bf16[128,1024]{1,0:T(8,128)(2,1)S(1)}, bf16[128,1024]{1,0:T(8,128)(2,1)S(1)}, u32[]{:S(2)}, u32[]{:S(2)}) collective-permute-start(bf16[128,1024]{1,0:T(8,128)(2,1)S(1)} %get-tuple-element.26), channel_id=1, source_target_pairs={{0,8},{1,9},{8,0},{9,1},{16,24},{17,25},{24,16},{25,17},{2,10},{3,... | collective-permute-start | bytes 786440 | tf_op jit(solution)/shard_map/ppermute | solution.py:256
  178.5 2.1 %collective-permute-start.16 = (bf16[128,1024]{1,0:T(8,128)(2,1)S(1)}, bf16[128,1024]{1,0:T(8,128)(2,1)S(1)}, u32[]{:S(2)}, u32[]{:S(2)}) collective-permute-start(bf16[128,1024]{1,0:T(8,128)(2,1)S(1)} %get-tuple-element.29), channel_id=1, source_target_pairs={{0,24},{1,25},{8,16},{9,17},{16,8},{17,9},{24,0},{25,1},{2,26},{3,... | collective-permute-start | bytes 786440 | tf_op jit(solution)/shard_map/ppermute | solution.py:256
  180.6 1.4 collective-permute-start.14
  182.2 1.3 collective-permute-start.15
  183.6 2.0 collective-permute-done.12
  186.3 4.5 %collective-permute-done.13 = bf16[128,1024]{1,0:T(8,128)(2,1)S(1)} collective-permute-done((bf16[128,1024]{1,0:T(8,128)(2,1)S(1)}, bf16[128,1024]{1,0:T(8,128)(2,1)S(1)}, u32[]{:S(2)}, u32[]{:S(2)}) %collective-permute-start.13) | collective-permute-done | bytes 262176 | tf_op jit(solution)/shard_map/ppermute | solution.py:256
  190.8 7.7 %collective-permute-done.14 = bf16[128,1024]{1,0:T(8,128)(2,1)S(1)} collective-permute-done((bf16[128,1024]{1,0:T(8,128)(2,1)S(1)}, bf16[128,1024]{1,0:T(8,128)(2,1)S(1)}, u32[]{:S(2)}, u32[]{:S(2)}) %collective-permute-start.14) | collective-permute-done | bytes 262176 | tf_op jit(solution)/shard_map/ppermute | solution.py:256
  198.5 4.4 %collective-permute-done.15 = bf16[128,1024]{1,0:T(8,128)(2,1)S(1)} collective-permute-done((bf16[128,1024]{1,0:T(8,128)(2,1)S(1)}, bf16[128,1024]{1,0:T(8,128)(2,1)S(1)}, u32[]{:S(2)}, u32[]{:S(2)}) %collective-permute-start.15) | collective-permute-done | bytes 262176 | tf_op jit(solution)/shard_map/ppermute | solution.py:256
  203.0 3.1 %collective-permute-done.17 = bf16[128,1024]{1,0:T(8,128)(2,1)S(1)} collective-permute-done((bf16[128,1024]{1,0:T(8,128)(2,1)S(1)}, bf16[128,1024]{1,0:T(8,128)(2,1)S(1)}, u32[]{:S(2)}, u32[]{:S(2)}) %collective-permute-start.17) | collective-permute-done | bytes 262176 | tf_op jit(solution)/shard_map/ppermute | solution.py:256
  (112 shorter events, 12.6 us)
Async XLA Ops:
  0.0 101.8 %copy-start = (s32[4,16,4]{1,2,0:T(4,128)S(1)}, s32[4,16,4]{1,2,0:T(4,128)}, u32[]{:S(2)}) copy-start(s32[4,16,4]{1,2,0:T(4,128)} %param.15) | copy-start | bytes 3076
  2.0 16.3 %all-to-all-start = ((bf16[8,288,128]{2,1,0:T(8,128)(2,1)}), bf16[8,288,128]{2,1,0:T(8,128)(2,1)S(1)}, u32[]{:S(2)}, u32[]{:S(2)}) async-start(bf16[8,288,128]{2,1,0:T(8,128)(2,1)} %packing.1), calls=%async_computation | async-start | bytes 1179648 | tf_op jit(solution)/shard_map/all_to_all | solution.py:318
  18.4 25.1 %copy-start.1 = (bf16[8,288,128]{2,1,0:T(8,128)(2,1)}, bf16[8,288,128]{2,1,0:T(8,128)(2,1)S(1)}, u32[]{:S(2)}) copy-start(bf16[8,288,128]{2,1,0:T(8,128)(2,1)S(1)} %all-to-all-done.refs_2_.own0) | copy-start | bytes 1769476
  18.4 14.8 %collective-permute-start.4 = (bf16[8,288,128]{2,1,0:T(8,128)(2,1)S(1)}, bf16[8,288,128]{2,1,0:T(8,128)(2,1)S(1)}, u32[]{:S(2)}, u32[]{:S(2)}) collective-permute-start(bf16[8,288,128]{2,1,0:T(8,128)(2,1)S(1)} %all-to-all-done.refs_2_.own0), channel_id=1, source_target_pairs={{0,2},{2,4},{4,6},{6,0},{1,3},{3,5},{5,7},{7,1},{8,10},{10,12},{12... | collective-permute-start | bytes 1769480 | tf_op jit(solution)/shard_map/ppermute | solution.py:252
  18.6 16.1 %collective-permute-start.6 = (bf16[8,288,128]{2,1,0:T(8,128)(2,1)S(1)}, bf16[8,288,128]{2,1,0:T(8,128)(2,1)S(1)}, u32[]{:S(2)}, u32[]{:S(2)}) collective-permute-start(bf16[8,288,128]{2,1,0:T(8,128)(2,1)S(1)} %all-to-all-done.refs_2_.own0), channel_id=1, source_target_pairs={{0,6},{2,0},{4,2},{6,4},{1,7},{3,1},{5,3},{7,5},{8,14},{10,8},{12,... | collective-permute-start | bytes 1769480 | tf_op jit(solution)/shard_map/ppermute | solution.py:252
  33.1 10.4 %copy-start.3 = (bf16[8,288,128]{2,1,0:T(8,128)(2,1)}, bf16[8,288,128]{2,1,0:T(8,128)(2,1)S(1)}, u32[]{:S(2)}) copy-start(bf16[8,288,128]{2,1,0:T(8,128)(2,1)S(1)} %collective-permute-done.4.refs_3_.own1) | copy-start | bytes 1769476
  33.2 7.7 %collective-permute-start.5 = (bf16[4,288,128]{2,1,0:T(8,128)(2,1)S(1)}, bf16[4,288,128]{2,1,0:T(8,128)(2,1)S(1)}, u32[]{:S(2)}, u32[]{:S(2)}) collective-permute-start(bf16[4,288,128]{2,1,0:T(8,128)(2,1)S(1)} %slice.16), channel_id=1, source_target_pairs={{0,2},{2,4},{4,6},{6,0},{1,3},{3,5},{5,7},{7,1},{8,10},{10,12},{12... | collective-permute-start | bytes 884744 | tf_op jit(solution)/shard_map/ppermute | solution.py:252
  34.7 8.8 %copy-start.5 = (bf16[8,288,128]{2,1,0:T(8,128)(2,1)}, bf16[8,288,128]{2,1,0:T(8,128)(2,1)S(1)}, u32[]{:S(2)}) copy-start(bf16[8,288,128]{2,1,0:T(8,128)(2,1)S(1)} %collective-permute-done.6.refs_5_.own3) | copy-start | bytes 1769476
  34.8 8.7 %collective-permute-start.7 = (bf16[4,288,128]{2,1,0:T(8,128)(2,1)S(1)}, bf16[4,288,128]{2,1,0:T(8,128)(2,1)S(1)}, u32[]{:S(2)}, u32[]{:S(2)}) collective-permute-start(bf16[4,288,128]{2,1,0:T(8,128)(2,1)S(1)} %slice.17), channel_id=1, source_target_pairs={{0,6},{2,0},{4,2},{6,4},{1,7},{3,1},{5,3},{7,5},{8,14},{10,8},{12,... | collective-permute-start | bytes 884744 | tf_op jit(solution)/shard_map/ppermute | solution.py:252
  78.0 43.9 %all-to-all-start.1 = ((bf16[8,2,256,128]{3,2,1,0:T(8,128)(2,1)}), bf16[8,2,256,128]{3,2,1,0:T(8,128)(2,1)S(1)}, u32[]{:S(2)}, u32[]{:S(2)}) async-start(bf16[8,2,256,128]{3,2,1,0:T(8,128)(2,1)} %picking.1), calls=%async_computation.1 | async-start | bytes 2097152 | tf_op jit(solution)/shard_map/all_to_all | solution.py:340
  82.7 22.2 %copy-start.2 = (bf16[8,288,128]{2,1,0:T(8,128)(2,1)S(1)}, bf16[8,288,128]{2,1,0:T(8,128)(2,1)}, u32[]{:S(2)}) copy-start(bf16[8,288,128]{2,1,0:T(8,128)(2,1)} %copy-done.1) | copy-start | bytes 1769476
  82.7 22.3 %copy-start.4 = (bf16[8,288,128]{2,1,0:T(8,128)(2,1)S(1)}, bf16[8,288,128]{2,1,0:T(8,128)(2,1)}, u32[]{:S(2)}) copy-start(bf16[8,288,128]{2,1,0:T(8,128)(2,1)} %copy-done.3) | copy-start | bytes 1769476
  82.7 22.3 %copy-start.6 = (bf16[8,288,128]{2,1,0:T(8,128)(2,1)S(1)}, bf16[8,288,128]{2,1,0:T(8,128)(2,1)}, u32[]{:S(2)}) copy-start(bf16[8,288,128]{2,1,0:T(8,128)(2,1)} %copy-done.5) | copy-start | bytes 1769476
  82.7 22.3 %copy-start.8 = (bf16[8,288,128]{2,1,0:T(8,128)(2,1)S(1)}, bf16[8,288,128]{2,1,0:T(8,128)(2,1)}, u32[]{:S(2)}) copy-start(bf16[8,288,128]{2,1,0:T(8,128)(2,1)} %copy-done.7) | copy-start | bytes 1769476
  85.6 9.2 %collective-permute-start.1 = (bf16[128,1024]{1,0:T(8,128)(2,1)S(1)}, bf16[128,1024]{1,0:T(8,128)(2,1)S(1)}, u32[]{:S(2)}, u32[]{:S(2)}) collective-permute-start(bf16[128,1024]{1,0:T(8,128)(2,1)S(1)} %get-tuple-element.43), channel_id=1, source_target_pairs={{0,8},{1,9},{8,0},{9,1},{16,24},{17,25},{24,16},{25,17},{2,10},{3,... | collective-permute-start | bytes 786440 | tf_op jit(solution)/shard_map/ppermute | solution.py:256
  86.2 14.9 %collective-permute-start.3 = (bf16[128,1024]{1,0:T(8,128)(2,1)S(1)}, bf16[128,1024]{1,0:T(8,128)(2,1)S(1)}, u32[]{:S(2)}, u32[]{:S(2)}) collective-permute-start(bf16[128,1024]{1,0:T(8,128)(2,1)S(1)} %get-tuple-element.41), channel_id=1, source_target_pairs={{0,16},{1,17},{8,24},{9,25},{16,0},{17,1},{24,8},{25,9},{2,18},{3,... | collective-permute-start | bytes 786440 | tf_op jit(solution)/shard_map/ppermute | solution.py:256
  88.3 33.5 %collective-permute-start.2 = (bf16[128,1024]{1,0:T(8,128)(2,1)}, bf16[128,1024]{1,0:T(8,128)(2,1)}, u32[]{:S(2)}, u32[]{:S(2)}) collective-permute-start(bf16[128,1024]{1,0:T(8,128)(2,1)} %get-tuple-element.42), channel_id=1, source_target_pairs={{0,9},{1,8},{8,1},{9,0},{16,25},{17,24},{24,17},{25,16},{2,11},{3,... | collective-permute-start | bytes 786440 | tf_op jit(solution)/shard_map/ppermute | solution.py:256
  88.4 33.4 %collective-permute-start.8 = (bf16[128,1024]{1,0:T(8,128)(2,1)}, bf16[128,1024]{1,0:T(8,128)(2,1)}, u32[]{:S(2)}, u32[]{:S(2)}) collective-permute-start(bf16[128,1024]{1,0:T(8,128)(2,1)} %get-tuple-element.40), channel_id=1, source_target_pairs={{0,17},{1,16},{8,25},{9,24},{16,1},{17,0},{24,9},{25,8},{2,19},{3,... | collective-permute-start | bytes 786440 | tf_op jit(solution)/shard_map/ppermute | solution.py:256
  91.6 53.4 %collective-permute-start = (bf16[128,1024]{1,0:T(8,128)(2,1)}, bf16[128,1024]{1,0:T(8,128)(2,1)}, u32[]{:S(2)}, u32[]{:S(2)}) collective-permute-start(bf16[128,1024]{1,0:T(8,128)(2,1)} %get-tuple-element.44), channel_id=1, source_target_pairs={{0,24},{1,25},{8,16},{9,17},{16,8},{17,9},{24,0},{25,1},{2,26},{3,... | collective-permute-start | bytes 786440 | tf_op jit(solution)/shard_map/ppermute | solution.py:256
  95.5 64.5 %collective-permute-start.9 = (bf16[128,1024]{1,0:T(8,128)(2,1)}, bf16[128,1024]{1,0:T(8,128)(2,1)}, u32[]{:S(2)}, u32[]{:S(2)}) collective-permute-start(bf16[128,1024]{1,0:T(8,128)(2,1)} %get-tuple-element.38), channel_id=1, source_target_pairs={{0,25},{1,24},{8,17},{9,16},{16,9},{17,8},{24,1},{25,0},{2,27},{3,... | collective-permute-start | bytes 786440 | tf_op jit(solution)/shard_map/ppermute | solution.py:256
  101.8 58.2 %collective-permute-start.10 = (bf16[128,1024]{1,0:T(8,128)(2,1)}, bf16[128,1024]{1,0:T(8,128)(2,1)}, u32[]{:S(2)}, u32[]{:S(2)}) collective-permute-start(bf16[128,1024]{1,0:T(8,128)(2,1)} %get-tuple-element.37), channel_id=1, source_target_pairs={{0,1},{1,0},{8,9},{9,8},{16,17},{17,16},{24,25},{25,24},{2,3},{3,2... | collective-permute-start | bytes 786440 | tf_op jit(solution)/shard_map/ppermute | solution.py:256
  121.8 17.9 %copy-start.12 = (bf16[128,1024]{1,0:T(8,128)(2,1)S(1)}, bf16[128,1024]{1,0:T(8,128)(2,1)}, u32[]{:S(2)}) copy-start(bf16[128,1024]{1,0:T(8,128)(2,1)} %copy-done.10) | copy-start | bytes 786436
  121.8 17.9 %copy-start.15 = (bf16[128,1024]{1,0:T(8,128)(2,1)S(1)}, bf16[128,1024]{1,0:T(8,128)(2,1)}, u32[]{:S(2)}) copy-start(bf16[128,1024]{1,0:T(8,128)(2,1)} %copy-done.13) | copy-start | bytes 786436
  121.8 17.9 %copy-start.17 = (f32[152,1024]{1,0:T(8,128)S(1)}, f32[152,1024]{1,0:T(8,128)}, u32[]{:S(2)}) copy-start(f32[152,1024]{1,0:T(8,128)} %copy-done.16) | copy-start | bytes 1867780
  121.8 17.9 %copy-start.19 = (f32[152,1024]{1,0:T(8,128)S(1)}, f32[152,1024]{1,0:T(8,128)}, u32[]{:S(2)}) copy-start(f32[152,1024]{1,0:T(8,128)} %copy-done.18) | copy-start | bytes 1867780
  174.9 7.4 %collective-permute-start.11 = (bf16[128,1024]{1,0:T(8,128)(2,1)S(1)}, bf16[128,1024]{1,0:T(8,128)(2,1)S(1)}, u32[]{:S(2)}, u32[]{:S(2)}) collective-permute-start(bf16[128,1024]{1,0:T(8,128)(2,1)S(1)} %get-tuple-element.31), channel_id=1, source_target_pairs={{0,1},{1,0},{8,9},{9,8},{16,17},{17,16},{24,25},{25,24},{2,3},{3,2... | collective-permute-start | bytes 786440 | tf_op jit(solution)/shard_map/ppermute | solution.py:256
  175.5 10.2 %collective-permute-start.12 = (bf16[128,1024]{1,0:T(8,128)(2,1)S(1)}, bf16[128,1024]{1,0:T(8,128)(2,1)S(1)}, u32[]{:S(2)}, u32[]{:S(2)}) collective-permute-start(bf16[128,1024]{1,0:T(8,128)(2,1)S(1)} %get-tuple-element.26), channel_id=1, source_target_pairs={{0,8},{1,9},{8,0},{9,1},{16,24},{17,25},{24,16},{25,17},{2,10},{3,... | collective-permute-start | bytes 786440 | tf_op jit(solution)/shard_map/ppermute | solution.py:256
  178.5 12.3 %collective-permute-start.13 = (bf16[128,1024]{1,0:T(8,128)(2,1)S(1)}, bf16[128,1024]{1,0:T(8,128)(2,1)S(1)}, u32[]{:S(2)}, u32[]{:S(2)}) collective-permute-start(bf16[128,1024]{1,0:T(8,128)(2,1)S(1)} %get-tuple-element.23), channel_id=1, source_target_pairs={{0,9},{1,8},{8,1},{9,0},{16,25},{17,24},{24,17},{25,16},{2,11},{3,... | collective-permute-start | bytes 786440 | tf_op jit(solution)/shard_map/ppermute | solution.py:256
  178.5 24.5 %collective-permute-start.16 = (bf16[128,1024]{1,0:T(8,128)(2,1)S(1)}, bf16[128,1024]{1,0:T(8,128)(2,1)S(1)}, u32[]{:S(2)}, u32[]{:S(2)}) collective-permute-start(bf16[128,1024]{1,0:T(8,128)(2,1)S(1)} %get-tuple-element.29), channel_id=1, source_target_pairs={{0,24},{1,25},{8,16},{9,17},{16,8},{17,9},{24,0},{25,1},{2,26},{3,... | collective-permute-start | bytes 786440 | tf_op jit(solution)/shard_map/ppermute | solution.py:256
  180.6 17.9 %collective-permute-start.14 = (bf16[128,1024]{1,0:T(8,128)(2,1)S(1)}, bf16[128,1024]{1,0:T(8,128)(2,1)S(1)}, u32[]{:S(2)}, u32[]{:S(2)}) collective-permute-start(bf16[128,1024]{1,0:T(8,128)(2,1)S(1)} %get-tuple-element.32), channel_id=1, source_target_pairs={{0,16},{1,17},{8,24},{9,25},{16,0},{17,1},{24,8},{25,9},{2,18},{3,... | collective-permute-start | bytes 786440 | tf_op jit(solution)/shard_map/ppermute | solution.py:256
  182.2 20.7 %collective-permute-start.15 = (bf16[128,1024]{1,0:T(8,128)(2,1)S(1)}, bf16[128,1024]{1,0:T(8,128)(2,1)S(1)}, u32[]{:S(2)}, u32[]{:S(2)}) collective-permute-start(bf16[128,1024]{1,0:T(8,128)(2,1)S(1)} %get-tuple-element.33), channel_id=1, source_target_pairs={{0,17},{1,16},{8,25},{9,24},{16,1},{17,0},{24,9},{25,8},{2,19},{3,... | collective-permute-start | bytes 786440 | tf_op jit(solution)/shard_map/ppermute | solution.py:256
  185.6 20.5 %collective-permute-start.17 = (bf16[128,1024]{1,0:T(8,128)(2,1)S(1)}, bf16[128,1024]{1,0:T(8,128)(2,1)S(1)}, u32[]{:S(2)}, u32[]{:S(2)}) collective-permute-start(bf16[128,1024]{1,0:T(8,128)(2,1)S(1)} %get-tuple-element.34), channel_id=1, source_target_pairs={{0,25},{1,24},{8,17},{9,16},{16,9},{17,8},{24,1},{25,0},{2,27},{3,... | collective-permute-start | bytes 786440 | tf_op jit(solution)/shard_map/ppermute | solution.py:256
  (11 other events, 29.3 us)

commit v2 on v1

--- a/solution.py
+++ b/solution.py
@@ -21,10 +21,14 @@
 HIDDEN = -1e30
 OWN0, SIB0, DUMMY = 4, 36, 44
 VROWS = HD + 16
-SPAN = 8
+SPAN = 4
 QW = 512
 HALVES = GROUP // QW
 KB = SPAN * TOK
+
+
+def in_hbm(array):
+    return pltpu.with_memory_space_constraint(array, pltpu.HBM)
 
 
 def make_kernel(kind, chunks):
@@ -40,22 +44,26 @@
 
         queries = take(chunks)
         states = take(chunks) if kind == "close" else []
-        owns = take(4) if has_own else []
-        sibs = take(1) if has_sib else []
+        owns = take(4) if kind == "open" else []
+        sibs = take(1) if kind == "close" else []
+        kbuf, vbuf = take(2) if kind != "open" else (None, None)
         outs = take(chunks)
-        kbuf, vbuf, past, todo, q_t, s_buf, p_buf, a_buf, acc, top, sem = refs
+        if kind != "full":
+            kbuf, vbuf = take(2)
+        todo, q_t, s_buf, p_buf, a_buf, acc, top = take(7)
+        past = take(1)[0] if kind == "open" else None
+        sem = take(1)[0] if kind != "full" else None
         step = pl.program_id(0)
         chunk_z, chunk_core, y = plan[0, step], plan[1, step], plan[2, step]
 
-        @pl.when(step == 0)
-        def _():
+        def fill():
             pairs = []
             for r, own in enumerate(owns):
                 here = pl.ds(OWN0 + 8 * r, 8)
                 pairs.append((own.at[:, pl.ds(0, TOK)], kbuf.at[here]))
                 pairs.append((own.at[:, pl.ds(TOK, HD)], vbuf.at[here, pl.ds(0, HD)]))
                 pairs.append((own.at[:, pl.ds(TOK + HD, 2 * PAST)], past.at[r]))
-            for slot in range(NSIB if has_sib else 0):
+            for slot in range(NSIB if sibs else 0):
                 source = sibs[0].at[plan[3 + NSIB + slot, 0]]
                 here = pl.ds(SIB0 + 2 * slot, 2)
                 pairs.append((source.at[:, pl.ds(0, TOK)], kbuf.at[here]))
@@ -63,16 +71,22 @@
             copies = [pltpu.make_async_copy(a, b, sem.at[i]) for i, (a, b) in enumerate(pairs)]
             for copy in copies:
                 copy.start()
-            row = lax.broadcasted_iota(jnp.int32, (VROWS - HD, TOK), 0)
-            ones = jnp.where(row == 0, 1.0, 0.0).astype(jnp.bfloat16)
-            for t in range(DUMMY):
-                vbuf[t, HD:VROWS, :] = ones
-            vbuf[DUMMY] = jnp.zeros((VROWS, TOK), jnp.bfloat16)
+            if owns:
+                row = lax.broadcasted_iota(jnp.int32, (VROWS - HD, TOK), 0)
+                ones = jnp.where(row == 0, 1.0, 0.0).astype(jnp.bfloat16)
+                for t in range(DUMMY):
+                    vbuf[t, HD:VROWS, :] = ones
+                vbuf[DUMMY] = jnp.zeros((VROWS, TOK), jnp.bfloat16)
             for copy in copies:
                 copy.wait()
             for r in range(len(owns)):
                 kbuf[r] = past[r, :, 0:PAST].reshape(TOK, HD)
                 vbuf[r, 0:HD] = past[r, :, PAST : 2 * PAST].reshape(TOK, HD).T
+            if owns:
+                kbuf[DUMMY] = kbuf[0]
+
+        if kind != "full":
+            pl.when(step == 0)(fill)
 
         def load(ref):
             for h in range(KVH):
@@ -115,10 +129,8 @@
                 todo[n] = SIB0 + 2 * slot
                 todo[n + 1] = SIB0 + 2 * slot + 1
                 n = n + jnp.where(plan[3 + slot, step] == 1, 2, 0)
-        repeat = todo[1 if has_own else 0]
         for t in range(2 * SPAN):
             todo[n + t] = DUMMY
-        kbuf[DUMMY] = kbuf[repeat]
         groups = lax.div(n + SPAN - 1, SPAN)
 
         def score(j, g):
@@ -183,13 +195,15 @@
             lax.fori_loop(1, groups, turn, 0)
             gather(groups - 1, last)
         else:
-            @pl.when(groups > 0)
-            def _():
+            def listed(j, carry):
                 for g in range(HALVES):
-                    score(0, g)
+                    score(j, g)
                 for g in range(HALVES):
                     weigh(g)
-                    gather(0, g)
+                    gather(j, g)
+                return carry
+
+            lax.fori_loop(0, groups, listed, 0)
 
         def store(ref):
             if kind == "open":
@@ -209,42 +223,52 @@
     return kernel
 
 
-def attend(kind, plan, queries, states, owns, sib):
+def attend(kind, plan, queries, states, source, buffers):
     chunks = len(queries)
 
     def whole(a):
         return pl.BlockSpec(a.shape, lambda i, plan: (0,) * a.ndim, pipeline_mode=pl.Buffered(1))
 
     blocked = [*queries, *(states if kind == "close" else ())]
-    raw = [*(owns if kind != "close" else ()), *((sib,) if kind != "open" else ())]
+    raw = list(source) if kind != "full" else []
+    kept = list(buffers) if kind != "open" else []
     if kind == "open":
         result = jax.ShapeDtypeStruct((VROWS + 8, GROUP), jnp.float32)
     else:
         result = jax.ShapeDtypeStruct((TOK, GROUP), jnp.bfloat16)
+    tile_shapes = [(DUMMY + 1, TOK, HD), (DUMMY + 1, VROWS, TOK)]
+    tiles = [jax.ShapeDtypeStruct(shape, jnp.bfloat16) for shape in tile_shapes] if kind != "full" else []
+    resident = pl.BlockSpec(memory_space=pltpu.VMEM)
+    scratch = [
+        pltpu.SMEM((72,), jnp.int32),
+        pltpu.VMEM((2 * HD, GROUP), jnp.bfloat16),
+        pltpu.VMEM((HALVES, KB, QW), jnp.float32),
+        pltpu.VMEM((HALVES, KB, QW), jnp.bfloat16),
+        pltpu.VMEM((1, GROUP), jnp.float32),
+        pltpu.VMEM((VROWS, GROUP), jnp.float32),
+        pltpu.VMEM((1, GROUP), jnp.float32),
+    ]
+    if kind == "open":
+        scratch.append(pltpu.VMEM((4, 8, 2 * PAST, HD), jnp.bfloat16))
+    if kind != "full":
+        scratch.append(pltpu.SemaphoreType.DMA((16,)))
+    first_kept = 1 + len(blocked) + len(raw)
+    aliases = {first_kept: chunks, first_kept + 1: chunks + 1} if kind == "close" else {}
     return pl.pallas_call(
         make_kernel(kind, chunks),
-        out_shape=(result,) * chunks,
+        out_shape=(result,) * chunks + tuple(tiles),
         grid_spec=pltpu.PrefetchScalarGridSpec(
             num_scalar_prefetch=1,
             grid=(chunks,),
-            in_specs=[whole(a) for a in blocked] + [pl.BlockSpec(memory_space=pl.ANY)] * len(raw),
-            out_specs=[pl.BlockSpec(result.shape, lambda i, plan: (0, 0))] * chunks,
-            scratch_shapes=[
-                pltpu.VMEM((DUMMY + 1, TOK, HD), jnp.bfloat16),
-                pltpu.VMEM((DUMMY + 1, VROWS, TOK), jnp.bfloat16),
-                pltpu.VMEM((4, 8, 2 * PAST, HD), jnp.bfloat16),
-                pltpu.SMEM((72,), jnp.int32),
-                pltpu.VMEM((2 * HD, GROUP), jnp.bfloat16),
-                pltpu.VMEM((HALVES, KB, QW), jnp.float32),
-                pltpu.VMEM((HALVES, KB, QW), jnp.bfloat16),
-                pltpu.VMEM((1, GROUP), jnp.float32),
-                pltpu.VMEM((VROWS, GROUP), jnp.float32),
-                pltpu.VMEM((1, GROUP), jnp.float32),
-                pltpu.SemaphoreType.DMA((20,)),
-            ],
+            in_specs=[whole(a) for a in blocked]
+            + [pl.BlockSpec(memory_space=pltpu.HBM)] * len(raw)
+            + [resident] * len(kept),
+            out_specs=[pl.BlockSpec(result.shape, lambda i, plan: (0, 0))] * chunks + [resident] * len(tiles),
+            scratch_shapes=scratch,
         ),
-        compiler_params=pltpu.CompilerParams(vmem_limit_bytes=32 * 2**20),
-    )(plan, *blocked, *raw)
+        input_output_aliases=aliases,
+        compiler_params=pltpu.CompilerParams(vmem_limit_bytes=24 * 2**20),
+    )(plan, *[in_hbm(a) for a in blocked], *[in_hbm(a) for a in raw], *kept)
 
 
 def shifted(value, axis, by):
@@ -274,39 +298,32 @@
     return pl.pallas_call(packing, out_shape=shape, name="packing")(*arrays)
 
 
-def picking(where, own0, own1, own2, own3, out_ref, sem):
+def picking(where, own0, own1, own2, own3, out_ref):
     count = out_ref.shape[0]
-
-    def copy(own, e):
-        pair = own.at[pl.ds(2 * where[count + e], 2), pl.ds(0, TOK + HD)]
-        return pltpu.make_async_copy(pair, out_ref.at[e], sem.at[e])
-
     for e in range(count):
         for r, own in enumerate((own0, own1, own2, own3)):
 
             @pl.when(where[e] == r)
             def _(own=own, e=e):
-                copy(own, e).start()
-
-    for e in range(count):
-        copy(own0, e).wait()
+                out_ref[e] = own[pl.ds(2 * where[count + e], 2), 0 : TOK + HD]
 
 
 def picked(where, owns):
     entries = where.shape[0] // 2
-    raw = pl.BlockSpec(memory_space=pl.ANY)
+    shape = (entries, 2, TOK + HD, HD)
+    whole = pl.BlockSpec(owns[0].shape, lambda i, where: (0, 0, 0), pipeline_mode=pl.Buffered(1))
     return pl.pallas_call(
         picking,
-        out_shape=jax.ShapeDtypeStruct((entries, 2, TOK + HD, HD), jnp.bfloat16),
+        out_shape=jax.ShapeDtypeStruct(shape, jnp.bfloat16),
         grid_spec=pltpu.PrefetchScalarGridSpec(
             num_scalar_prefetch=1,
             grid=(1,),
-            in_specs=[raw] * 4,
-            out_specs=raw,
-            scratch_shapes=[pltpu.SemaphoreType.DMA((entries,))],
+            in_specs=[whole] * 4,
+            out_specs=pl.BlockSpec(shape, lambda i, where: (0, 0, 0, 0), pipeline_mode=pl.Buffered(1)),
         ),
+        compiler_params=pltpu.CompilerParams(vmem_limit_bytes=16 * 2**20),
         name="picking",
-    )(where, *owns)
+    )(where, *[in_hbm(own) for own in owns])
 
 
 def attention(query, key_new, value_new, hist_key, hist_value, sib_source, sib_block, sib_mask):
@@ -350,12 +367,15 @@
         rows.append(jnp.broadcast_to(flat[:, None], (NSIB, len(steps))))
         return jnp.concatenate(rows, axis=0).astype(jnp.int32)
 
-    parts, states, previous = {}, {}, None
+    parts, states, previous, buffers = {}, {}, None, ()
     for kind, steps in CALLS:
         asked = [queries[s] for s in steps]
         if previous is not None:
             asked[0] = after(asked[0], previous)
-        results = attend(kind, plan_of(steps), asked, [states.get(s) for s in steps], owns, sib)
+        source = owns if kind == "open" else (sib,)
+        results = attend(kind, plan_of(steps), asked, [states.get(s) for s in steps], source, buffers)
+        if kind != "full":
+            buffers = results[len(steps) :]
         previous = results[0]
         for s, result in zip(steps, results):
             if kind == "open":
@@ -369,7 +389,7 @@
 
 
 QORDER = (2, 4, 3, 5, 6, 7, 1, 0)
-CALLS = (("open", (2, 4)), ("full", (3, 5)), ("close", (2, 4)), ("full", (6, 0)), ("full", (7, 1)))
+CALLS = (("open", (2, 4)), ("close", (2, 4)), ("full", (3, 5)), ("full", (6, 0)), ("full", (7, 1)))
 
 
 def solution(mesh):
@@ -385,6 +405,4 @@
         P(),
         P(),
     )
-    return jax.shard_map(
-        attention, mesh=split, in_specs=placed, out_specs=P("branch", seq, None), check_vma=False
-    )
+    return jax.shard_map(attention, mesh=split, in_specs=placed, out_specs=P("branch", seq, None), check_vma=False)

time: 207 us -> 173 us (0.84)
  Pallas kernels: 102 us -> 72.6 us
  local copies, waits for them, and re-layouts: 13.2 us -> 8.15 us
    pallas_call x6, Pallas kernels: 99.7 us -> 70.6 us  [the longest x5 67.2 us: attend(): pl.pallas_call(make_kernel(kind, chunks), out_shape=(result,) * chunks +...]
    unnamed x47 -> x25, local copies, waits for them, and re-layouts: 5.9 us -> 2.52 us
  transfers between devices with their start and end apart: 20 -> 20, of which waited for: 11 -> 11; matrix products, arithmetic and copies ran while one was open for 4% -> 3% of each run, Pallas kernels for 25% -> 31%
where the time goes in v2:
time: 173 us; the launch traced here: 172 us
  Pallas kernels  72.6 us (42%)
  waiting for transfers between devices  61.4 us (35%)
  starting transfers between devices  29.1 us (17%)
  local copies, waits for them, and re-layouts  8.15 us (5%)
    pallas_call x5, Pallas kernels, attend(): pl.pallas_call(make_kernel(kind, chunks), out_shape=(result,) * chunks +...  67.2 us
    ppermute x14, waiting for transfers between devices, exchanged(): return lax.ppermute(value, (Z, CORE), [(k, k ^ step) for k in range(8)])  30.8 us
    ppermute x4, waiting for transfers between devices, shifted(): return lax.ppermute(value, axis, [(k, (k + by) % n) for k in range(n)])  20.1 us
    ppermute x14, starting transfers between devices, exchanged(): return lax.ppermute(value, (Z, CORE), [(k, k ^ step) for k in range(8)])  14.6 us
    all_to_all x1, waiting for transfers between devices, attention(): lax.all_to_all(send, (Z, CORE), split_axis=0, concat_axis=0, tiled=True)  10.5 us
    all_to_all x1, starting transfers between devices, attention(): lax.all_to_all(send, (Z, CORE), split_axis=0, concat_axis=0, tiled=True)  5.31 us
    all_to_all x1, starting transfers between devices, attention(): lax.all_to_all(sent, 'branch', split_axis=0, concat_axis=0, tiled=True)  4.9 us
    ppermute x4, starting transfers between devices, shifted(): return lax.ppermute(value, axis, [(k, (k + by) % n) for k in range(n)])  4.26 us
  transfers between devices with their start and end apart: 20, of which 11 were waited for; matrix products, arithmetic and copies ran while one was open for 3% of the time, Pallas kernels for 31%

profile of v2, /device:TPU:30, one launch (start us, length us, event | category | flops | bytes accessed | tf_op | source)
XLA Modules:
  0.0 172.5 jit_solution(2057441290447334360)
XLA Ops:
  0.0 2.0 %packing.1 = bf16[8,288,128]{2,1,0:T(8,128)(2,1)} custom-call(bf16[1,128,1024]{2,1,0:T(8,128)(2,1)} %key_ref.1, bf16[1,128,1024]{2,1,0:T(8,128)(2,1)} %value_ref.1, bf16[16,1024]{1,0:T(8,128)(2,1)} %past_key_ref.1, bf16[16,1024]{1,0:T(8,128)(2,1)} %past_value_ref.1), custom_call_target="tpu_custom_call" | custom-call | tf_op jit(solution)/shard_map/packing/pallas_call | solution.py:298
  2.0 5.3 %all-to-all-start = ((bf16[8,288,128]{2,1,0:T(8,128)(2,1)}), bf16[8,288,128]{2,1,0:T(8,128)(2,1)S(1)}, u32[]{:S(2)}, u32[]{:S(2)}) async-start(bf16[8,288,128]{2,1,0:T(8,128)(2,1)} %packing.1), calls=%async_computation | async-start | bytes 1179648 | tf_op jit(solution)/shard_map/all_to_all | solution.py:335
  7.8 10.5 %all-to-all-done.refs_2_.own0 = bf16[8,288,128]{2,1,0:T(8,128)(2,1)S(1)} async-done(((bf16[8,288,128]{2,1,0:T(8,128)(2,1)}), bf16[8,288,128]{2,1,0:T(8,128)(2,1)S(1)}, u32[]{:S(2)}, u32[]{:S(2)}) %all-to-all-start) | async-done | bytes 589856 | tf_op jit(solution)/shard_map/all_to_all | solution.py:335
  18.6 1.9 %collective-permute-start.6 = (bf16[8,288,128]{2,1,0:T(8,128)(2,1)S(1)}, bf16[8,288,128]{2,1,0:T(8,128)(2,1)S(1)}, u32[]{:S(2)}, u32[]{:S(2)}) collective-permute-start(bf16[8,288,128]{2,1,0:T(8,128)(2,1)S(1)} %all-to-all-done.refs_2_.own0), channel_id=1, source_target_pairs={{0,6},{2,0},{4,2},{6,4},{1,7},{3,1},{5,3},{7,5},{8,14},{10,8},{12,... | collective-permute-start | bytes 1769480 | tf_op jit(solution)/shard_map/ppermute | solution.py:276
  20.8 12.3 %collective-permute-done.4.refs_3_.own1 = bf16[8,288,128]{2,1,0:T(8,128)(2,1)S(1)} collective-permute-done((bf16[8,288,128]{2,1,0:T(8,128)(2,1)S(1)}, bf16[8,288,128]{2,1,0:T(8,128)(2,1)S(1)}, u32[]{:S(2)}, u32[]{:S(2)}) %collective-permute-start.4) | collective-permute-done | bytes 589856 | tf_op jit(solution)/shard_map/ppermute | solution.py:276
  33.2 1.6 collective-permute-start.5
  35.6 5.2 %collective-permute-done.5 = bf16[4,288,128]{2,1,0:T(8,128)(2,1)S(1)} collective-permute-done((bf16[4,288,128]{2,1,0:T(8,128)(2,1)S(1)}, bf16[4,288,128]{2,1,0:T(8,128)(2,1)S(1)}, u32[]{:S(2)}, u32[]{:S(2)}) %collective-permute-start.5) | collective-permute-done | bytes 294944 | tf_op jit(solution)/shard_map/ppermute | solution.py:276
  40.8 2.6 %collective-permute-done.7 = bf16[4,288,128]{2,1,0:T(8,128)(2,1)S(1)} collective-permute-done((bf16[4,288,128]{2,1,0:T(8,128)(2,1)S(1)}, bf16[4,288,128]{2,1,0:T(8,128)(2,1)S(1)}, u32[]{:S(2)}, u32[]{:S(2)}) %collective-permute-start.7) | collective-permute-done | bytes 294944 | tf_op jit(solution)/shard_map/ppermute | solution.py:276
  43.5 0.8 copy-done.6
  44.3 3.4 %picking.1 = bf16[8,2,256,128]{3,2,1,0:T(8,128)(2,1)} custom-call(s32[16]{0:T(128)S(1)} %pad_add_fusion.7.where, bf16[8,288,128]{2,1,0:T(8,128)(2,1)} %copy-done.3, bf16[8,288,128]{2,1,0:T(8,128)(2,1)} %copy-done.4, bf16[8,288,128]{2,1,0:T(8,128)(2,1)} %copy-done.6, bf16[8,288,128]{2,1,0:T(8,128)(2,1)} %copy-done.5), custom_call_target="tpu_custom_call" | custom-call | tf_op jit(solution)/shard_map/picking/pallas_call | solution.py:315
  47.7 4.9 %all-to-all-start.1 = ((bf16[8,2,256,128]{3,2,1,0:T(8,128)(2,1)}), bf16[8,2,256,128]{3,2,1,0:T(8,128)(2,1)}, u32[]{:S(2)}, u32[]{:S(2)}) async-start(bf16[8,2,256,128]{3,2,1,0:T(8,128)(2,1)} %picking.1), calls=%async_computation.1 | async-start | bytes 2097152 | tf_op jit(solution)/shard_map/all_to_all | solution.py:357
  52.6 1.2 constant_dynamic-slice_fusion
  54.4 2.1 %collective-permute-start.3 = (bf16[128,1024]{1,0:T(8,128)(2,1)S(1)}, bf16[128,1024]{1,0:T(8,128)(2,1)}, u32[]{:S(2)}, u32[]{:S(2)}) collective-permute-start(bf16[128,1024]{1,0:T(8,128)(2,1)S(1)} %get-tuple-element.49), channel_id=1, source_target_pairs={{0,16},{1,17},{8,24},{9,25},{16,0},{17,1},{24,8},{25,9},{2,18},{3,... | collective-permute-start | bytes 786440 | tf_op jit(solution)/shard_map/ppermute | solution.py:280
  56.6 3.2 %collective-permute-start.8 = (bf16[128,1024]{1,0:T(8,128)(2,1)}, bf16[128,1024]{1,0:T(8,128)(2,1)}, u32[]{:S(2)}, u32[]{:S(2)}) collective-permute-start(bf16[128,1024]{1,0:T(8,128)(2,1)} %get-tuple-element.48), channel_id=1, source_target_pairs={{0,17},{1,16},{8,25},{9,24},{16,1},{17,0},{24,9},{25,8},{2,19},{3,... | collective-permute-start | bytes 786440 | tf_op jit(solution)/shard_map/ppermute | solution.py:280
  59.8 1.2 collective-permute-start
  61.0 2.0 %collective-permute-done.2.refs_0_ = bf16[128,1024]{1,0:T(8,128)(2,1)S(1)} collective-permute-done((bf16[128,1024]{1,0:T(8,128)(2,1)S(1)}, bf16[128,1024]{1,0:T(8,128)(2,1)S(1)}, u32[]{:S(2)}, u32[]{:S(2)}) %collective-permute-start.2) | collective-permute-done | bytes 262176 | tf_op jit(solution)/shard_map/ppermute | solution.py:280
  63.0 6.4 %collective-permute-done.3.refs_1_ = bf16[128,1024]{1,0:T(8,128)(2,1)} collective-permute-done((bf16[128,1024]{1,0:T(8,128)(2,1)S(1)}, bf16[128,1024]{1,0:T(8,128)(2,1)}, u32[]{:S(2)}, u32[]{:S(2)}) %collective-permute-start.3) | collective-permute-done | bytes 262176 | tf_op jit(solution)/shard_map/ppermute | solution.py:280
  72.6 14.3 %shard_map.82 = (f32[152,1024]{1,0:T(8,128)S(1)}, f32[152,1024]{1,0:T(8,128)S(1)}, bf16[45,128,128]{2,1,0:T(8,128)(2,1)S(1)}, bf16[45,144,128]{2,1,0:T(8,128)(2,1)S(1)}) custom-call(s32[11,2]{1,0:T(8,128)S(1)} %copy.41.plan, bf16[128,1024]{1,0:T(8,128)(2,1)} %copy-done.9, bf16[128,1024]{1,0:T(8,128)(2,1)} %collective-permute-done.3.refs_1_, ...), custom_call_target="tpu_custom_call" | custom-call | tf_op jit(solution)/shard_map/pallas_call | solution.py:257
  86.9 0.8 copy-done.1
  87.7 0.8 copy-done.2
  88.6 7.9 %shard_map.83 = (bf16[128,1024]{1,0:T(8,128)(2,1)S(1)}, bf16[128,1024]{1,0:T(8,128)(2,1)S(1)}, bf16[45,128,128]{2,1,0:T(8,128)(2,1)S(1)}, bf16[45,144,128]{2,1,0:T(8,128)(2,1)S(1)}) custom-call(s32[11,2]{1,0:T(8,128)S(1)} %copy.41.plan, bf16[128,1024]{1,0:T(8,128)(2,1)} %copy-done.9, ...), custom_call_target="tpu_custom_call", output_to_operand_aliasing={{2}: (6, {}), {3}: (7, {})} | custom-call | tf_op jit(solution)/shard_map/pallas_call | solution.py:257
  96.5 16.1 %shard_map.84 = (bf16[128,1024]{1,0:T(8,128)(2,1)S(1)}, bf16[128,1024]{1,0:T(8,128)(2,1)S(1)}) custom-call(s32[11,2]{1,0:T(8,128)S(1)} %copy.42.plan, bf16[128,1024]{1,0:T(8,128)(2,1)} %collective-permute-done.1.refs_0_, bf16[128,1024]{1,0:T(8,128)(2,1)} %collective-permute-done.8.refs_1_, bf16[45,128,128]{2,1,0:T(8,128)(2,1)S(1)} %get-tuple-element.32.refs_2_, ...), custom_call_target="tpu_custom_call" | custom-call | tf_op jit(solution)/shard_map/pallas_call | solution.py:257
  112.6 14.4 %shard_map.85 = (bf16[128,1024]{1,0:T(8,128)(2,1)S(1)}, bf16[128,1024]{1,0:T(8,128)(2,1)S(1)}) custom-call(s32[11,2]{1,0:T(8,128)S(1)} %copy.43.plan, bf16[128,1024]{1,0:T(8,128)(2,1)} %collective-permute-done.refs_0_, bf16[128,1024]{1,0:T(8,128)(2,1)} %get-tuple-element.47.refs_1_, bf16[45,128,128]{2,1,0:T(8,128)(2,1)S(1)} %get-tuple-element.32.refs_2_, ...), custom_call_target="tpu_custom_call" | custom-call | tf_op jit(solution)/shard_map/pallas_call | solution.py:257
  127.1 14.4 %shard_map.86 = (bf16[128,1024]{1,0:T(8,128)(2,1)S(1)}, bf16[128,1024]{1,0:T(8,128)(2,1)S(1)}) custom-call(s32[11,2]{1,0:T(8,128)S(1)} %copy.45.plan, bf16[128,1024]{1,0:T(8,128)(2,1)} %collective-permute-done.9.refs_0_, bf16[128,1024]{1,0:T(8,128)(2,1)} %collective-permute-done.10.refs_1_, bf16[45,128,128]{2,1,0:T(8,128)(2,1)S(1)} %get-tuple-element.32.refs_2_, ...), custom_call_target="tpu_custom_call" | custom-call | tf_op jit(solution)/shard_map/pallas_call | solution.py:257
  142.1 1.4 collective-permute-start.13
  143.6 2.1 %collective-permute-start.16 = (bf16[128,1024]{1,0:T(8,128)(2,1)S(1)}, bf16[128,1024]{1,0:T(8,128)(2,1)S(1)}, u32[]{:S(2)}, u32[]{:S(2)}) collective-permute-start(bf16[128,1024]{1,0:T(8,128)(2,1)S(1)} %get-tuple-element.37), channel_id=1, source_target_pairs={{0,24},{1,25},{8,16},{9,17},{16,8},{17,9},{24,0},{25,1},{2,26},{3,... | collective-permute-start | bytes 786440 | tf_op jit(solution)/shard_map/ppermute | solution.py:280
  146.5 2.8 %collective-permute-start.15 = (bf16[128,1024]{1,0:T(8,128)(2,1)S(1)}, bf16[128,1024]{1,0:T(8,128)(2,1)S(1)}, u32[]{:S(2)}, u32[]{:S(2)}) collective-permute-start(bf16[128,1024]{1,0:T(8,128)(2,1)S(1)} %get-tuple-element.41), channel_id=1, source_target_pairs={{0,17},{1,16},{8,25},{9,24},{16,1},{17,0},{24,9},{25,8},{2,19},{3,... | collective-permute-start | bytes 786440 | tf_op jit(solution)/shard_map/ppermute | solution.py:280
  149.3 2.0 %collective-permute-done.12 = bf16[128,1024]{1,0:T(8,128)(2,1)S(1)} collective-permute-done((bf16[128,1024]{1,0:T(8,128)(2,1)S(1)}, bf16[128,1024]{1,0:T(8,128)(2,1)S(1)}, u32[]{:S(2)}, u32[]{:S(2)}) %collective-permute-start.12) | collective-permute-done | bytes 262176 | tf_op jit(solution)/shard_map/ppermute | solution.py:280
  151.4 3.8 %collective-permute-done.13 = bf16[128,1024]{1,0:T(8,128)(2,1)S(1)} collective-permute-done((bf16[128,1024]{1,0:T(8,128)(2,1)S(1)}, bf16[128,1024]{1,0:T(8,128)(2,1)S(1)}, u32[]{:S(2)}, u32[]{:S(2)}) %collective-permute-start.13) | collective-permute-done | bytes 262176 | tf_op jit(solution)/shard_map/ppermute | solution.py:280
  155.2 8.9 %collective-permute-done.14 = bf16[128,1024]{1,0:T(8,128)(2,1)S(1)} collective-permute-done((bf16[128,1024]{1,0:T(8,128)(2,1)S(1)}, bf16[128,1024]{1,0:T(8,128)(2,1)S(1)}, u32[]{:S(2)}, u32[]{:S(2)}) %collective-permute-start.14) | collective-permute-done | bytes 262176 | tf_op jit(solution)/shard_map/ppermute | solution.py:280
  164.2 3.8 %collective-permute-done.15 = bf16[128,1024]{1,0:T(8,128)(2,1)S(1)} collective-permute-done((bf16[128,1024]{1,0:T(8,128)(2,1)S(1)}, bf16[128,1024]{1,0:T(8,128)(2,1)S(1)}, u32[]{:S(2)}, u32[]{:S(2)}) %collective-permute-start.15) | collective-permute-done | bytes 262176 | tf_op jit(solution)/shard_map/ppermute | solution.py:280
  168.1 3.7 %collective-permute-done.17 = bf16[128,1024]{1,0:T(8,128)(2,1)S(1)} collective-permute-done((bf16[128,1024]{1,0:T(8,128)(2,1)S(1)}, bf16[128,1024]{1,0:T(8,128)(2,1)S(1)}, u32[]{:S(2)}, u32[]{:S(2)}) %collective-permute-start.17) | collective-permute-done | bytes 262176 | tf_op jit(solution)/shard_map/ppermute | solution.py:280
  (90 shorter events, 8.1 us)
Async XLA Ops:
  0.0 69.4 %copy-start = (s32[4,16,4]{1,2,0:T(4,128)S(1)}, s32[4,16,4]{1,2,0:T(4,128)}, u32[]{:S(2)}) copy-start(s32[4,16,4]{1,2,0:T(4,128)} %param.15) | copy-start | bytes 3076
  0.0 7.3 %copy-start.10 = (s32[4,4]{1,0:T(4,128)S(1)}, s32[4,4]{1,0:T(4,128)}, u32[]{:S(2)}) copy-start(s32[4,4]{1,0:T(4,128)} %param.13) | copy-start | bytes 196
  0.0 7.7 %copy-start.11 = (s32[4,4]{1,0:T(4,128)S(1)}, s32[4,4]{1,0:T(4,128)}, u32[]{:S(2)}) copy-start(s32[4,4]{1,0:T(4,128)} %param.14) | copy-start | bytes 196
  2.0 16.3 %all-to-all-start = ((bf16[8,288,128]{2,1,0:T(8,128)(2,1)}), bf16[8,288,128]{2,1,0:T(8,128)(2,1)S(1)}, u32[]{:S(2)}, u32[]{:S(2)}) async-start(bf16[8,288,128]{2,1,0:T(8,128)(2,1)} %packing.1), calls=%async_computation | async-start | bytes 1179648 | tf_op jit(solution)/shard_map/all_to_all | solution.py:335
  18.4 25.1 %copy-start.3 = (bf16[8,288,128]{2,1,0:T(8,128)(2,1)}, bf16[8,288,128]{2,1,0:T(8,128)(2,1)S(1)}, u32[]{:S(2)}) copy-start(bf16[8,288,128]{2,1,0:T(8,128)(2,1)S(1)} %all-to-all-done.refs_2_.own0) | copy-start | bytes 1769476
  18.4 14.8 %collective-permute-start.4 = (bf16[8,288,128]{2,1,0:T(8,128)(2,1)S(1)}, bf16[8,288,128]{2,1,0:T(8,128)(2,1)S(1)}, u32[]{:S(2)}, u32[]{:S(2)}) collective-permute-start(bf16[8,288,128]{2,1,0:T(8,128)(2,1)S(1)} %all-to-all-done.refs_2_.own0), channel_id=1, source_target_pairs={{0,2},{2,4},{4,6},{6,0},{1,3},{3,5},{5,7},{7,1},{8,10},{10,12},{12... | collective-permute-start | bytes 1769480 | tf_op jit(solution)/shard_map/ppermute | solution.py:276
  18.6 16.1 %collective-permute-start.6 = (bf16[8,288,128]{2,1,0:T(8,128)(2,1)S(1)}, bf16[8,288,128]{2,1,0:T(8,128)(2,1)S(1)}, u32[]{:S(2)}, u32[]{:S(2)}) collective-permute-start(bf16[8,288,128]{2,1,0:T(8,128)(2,1)S(1)} %all-to-all-done.refs_2_.own0), channel_id=1, source_target_pairs={{0,6},{2,0},{4,2},{6,4},{1,7},{3,1},{5,3},{7,5},{8,14},{10,8},{12,... | collective-permute-start | bytes 1769480 | tf_op jit(solution)/shard_map/ppermute | solution.py:276
  33.1 10.4 %copy-start.4 = (bf16[8,288,128]{2,1,0:T(8,128)(2,1)}, bf16[8,288,128]{2,1,0:T(8,128)(2,1)S(1)}, u32[]{:S(2)}) copy-start(bf16[8,288,128]{2,1,0:T(8,128)(2,1)S(1)} %collective-permute-done.4.refs_3_.own1) | copy-start | bytes 1769476
  33.2 7.7 %collective-permute-start.5 = (bf16[4,288,128]{2,1,0:T(8,128)(2,1)S(1)}, bf16[4,288,128]{2,1,0:T(8,128)(2,1)S(1)}, u32[]{:S(2)}, u32[]{:S(2)}) collective-permute-start(bf16[4,288,128]{2,1,0:T(8,128)(2,1)S(1)} %slice.16), channel_id=1, source_target_pairs={{0,2},{2,4},{4,6},{6,0},{1,3},{3,5},{5,7},{7,1},{8,10},{10,12},{12... | collective-permute-start | bytes 884744 | tf_op jit(solution)/shard_map/ppermute | solution.py:276
  34.7 8.8 %copy-start.5 = (bf16[8,288,128]{2,1,0:T(8,128)(2,1)}, bf16[8,288,128]{2,1,0:T(8,128)(2,1)S(1)}, u32[]{:S(2)}) copy-start(bf16[8,288,128]{2,1,0:T(8,128)(2,1)S(1)} %collective-permute-done.6.refs_5_.own3) | copy-start | bytes 1769476
  34.8 8.7 %collective-permute-start.7 = (bf16[4,288,128]{2,1,0:T(8,128)(2,1)S(1)}, bf16[4,288,128]{2,1,0:T(8,128)(2,1)S(1)}, u32[]{:S(2)}, u32[]{:S(2)}) collective-permute-start(bf16[4,288,128]{2,1,0:T(8,128)(2,1)S(1)} %slice.17), channel_id=1, source_target_pairs={{0,6},{2,0},{4,2},{6,4},{1,7},{3,1},{5,3},{7,5},{8,14},{10,8},{12,... | collective-permute-start | bytes 884744 | tf_op jit(solution)/shard_map/ppermute | solution.py:276
  43.5 0.8 copy-start.6
  47.7 4.9 %copy-start.7 = (bf16[1,128,8192]{2,1,0:T(8,128)(2,1)S(1)}, bf16[1,128,8192]{2,1,0:T(8,128)(2,1)}, u32[]{:S(2)}) copy-start(bf16[1,128,8192]{2,1,0:T(8,128)(2,1)} %param.8) | copy-start | bytes 6291460
  47.7 40.9 %all-to-all-start.1 = ((bf16[8,2,256,128]{3,2,1,0:T(8,128)(2,1)}), bf16[8,2,256,128]{3,2,1,0:T(8,128)(2,1)}, u32[]{:S(2)}, u32[]{:S(2)}) async-start(bf16[8,2,256,128]{3,2,1,0:T(8,128)(2,1)} %picking.1), calls=%async_computation.1 | async-start | bytes 2097152 | tf_op jit(solution)/shard_map/all_to_all | solution.py:357
  53.8 9.2 %collective-permute-start.2 = (bf16[128,1024]{1,0:T(8,128)(2,1)S(1)}, bf16[128,1024]{1,0:T(8,128)(2,1)S(1)}, u32[]{:S(2)}, u32[]{:S(2)}) collective-permute-start(bf16[128,1024]{1,0:T(8,128)(2,1)S(1)} %get-tuple-element.50), channel_id=1, source_target_pairs={{0,8},{1,9},{8,0},{9,1},{16,24},{17,25},{24,16},{25,17},{2,10},{3,... | collective-permute-start | bytes 786440 | tf_op jit(solution)/shard_map/ppermute | solution.py:280
  54.4 15.0 %collective-permute-start.3 = (bf16[128,1024]{1,0:T(8,128)(2,1)S(1)}, bf16[128,1024]{1,0:T(8,128)(2,1)}, u32[]{:S(2)}, u32[]{:S(2)}) collective-permute-start(bf16[128,1024]{1,0:T(8,128)(2,1)S(1)} %get-tuple-element.49), channel_id=1, source_target_pairs={{0,16},{1,17},{8,24},{9,25},{16,0},{17,1},{24,8},{25,9},{2,18},{3,... | collective-permute-start | bytes 786440 | tf_op jit(solution)/shard_map/ppermute | solution.py:280
  56.5 40.0 %collective-permute-start.1 = (bf16[128,1024]{1,0:T(8,128)(2,1)}, bf16[128,1024]{1,0:T(8,128)(2,1)}, u32[]{:S(2)}, u32[]{:S(2)}) collective-permute-start(bf16[128,1024]{1,0:T(8,128)(2,1)} %get-tuple-element.51), channel_id=1, source_target_pairs={{0,9},{1,8},{8,1},{9,0},{16,25},{17,24},{24,17},{25,16},{2,11},{3,... | collective-permute-start | bytes 786440 | tf_op jit(solution)/shard_map/ppermute | solution.py:280
  56.6 40.0 %collective-permute-start.8 = (bf16[128,1024]{1,0:T(8,128)(2,1)}, bf16[128,1024]{1,0:T(8,128)(2,1)}, u32[]{:S(2)}, u32[]{:S(2)}) collective-permute-start(bf16[128,1024]{1,0:T(8,128)(2,1)} %get-tuple-element.48), channel_id=1, source_target_pairs={{0,17},{1,16},{8,25},{9,24},{16,1},{17,0},{24,9},{25,8},{2,19},{3,... | collective-permute-start | bytes 786440 | tf_op jit(solution)/shard_map/ppermute | solution.py:280
  59.8 52.8 %collective-permute-start = (bf16[128,1024]{1,0:T(8,128)(2,1)}, bf16[128,1024]{1,0:T(8,128)(2,1)}, u32[]{:S(2)}, u32[]{:S(2)}) collective-permute-start(bf16[128,1024]{1,0:T(8,128)(2,1)} %get-tuple-element.52), channel_id=1, source_target_pairs={{0,24},{1,25},{8,16},{9,17},{16,8},{17,9},{24,0},{25,1},{2,26},{3,... | collective-permute-start | bytes 786440 | tf_op jit(solution)/shard_map/ppermute | solution.py:280
  63.0 9.6 %copy-start.9 = (bf16[128,1024]{1,0:T(8,128)(2,1)}, bf16[128,1024]{1,0:T(8,128)(2,1)S(1)}, u32[]{:S(2)}) copy-start(bf16[128,1024]{1,0:T(8,128)(2,1)S(1)} %collective-permute-done.2.refs_0_) | copy-start | bytes 786436
  63.0 64.1 %collective-permute-start.9 = (bf16[128,1024]{1,0:T(8,128)(2,1)}, bf16[128,1024]{1,0:T(8,128)(2,1)}, u32[]{:S(2)}, u32[]{:S(2)}) collective-permute-start(bf16[128,1024]{1,0:T(8,128)(2,1)} %get-tuple-element.46), channel_id=1, source_target_pairs={{0,25},{1,24},{8,17},{9,16},{16,9},{17,8},{24,1},{25,0},{2,27},{3,... | collective-permute-start | bytes 786440 | tf_op jit(solution)/shard_map/ppermute | solution.py:280
  69.4 57.7 %collective-permute-start.10 = (bf16[128,1024]{1,0:T(8,128)(2,1)}, bf16[128,1024]{1,0:T(8,128)(2,1)}, u32[]{:S(2)}, u32[]{:S(2)}) collective-permute-start(bf16[128,1024]{1,0:T(8,128)(2,1)} %get-tuple-element.45), channel_id=1, source_target_pairs={{0,1},{1,0},{8,9},{9,8},{16,17},{17,16},{24,25},{25,24},{2,3},{3,2... | collective-permute-start | bytes 786440 | tf_op jit(solution)/shard_map/ppermute | solution.py:280
  86.9 0.8 copy-start.1
  87.7 0.8 copy-start.2
  141.5 5.0 %collective-permute-start.11 = (bf16[128,1024]{1,0:T(8,128)(2,1)S(1)}, bf16[128,1024]{1,0:T(8,128)(2,1)S(1)}, u32[]{:S(2)}, u32[]{:S(2)}) collective-permute-start(bf16[128,1024]{1,0:T(8,128)(2,1)S(1)} %get-tuple-element.39), channel_id=1, source_target_pairs={{0,1},{1,0},{8,9},{9,8},{16,17},{17,16},{24,25},{25,24},{2,3},{3,2... | collective-permute-start | bytes 786440 | tf_op jit(solution)/shard_map/ppermute | solution.py:280
  142.1 9.2 %collective-permute-start.12 = (bf16[128,1024]{1,0:T(8,128)(2,1)S(1)}, bf16[128,1024]{1,0:T(8,128)(2,1)S(1)}, u32[]{:S(2)}, u32[]{:S(2)}) collective-permute-start(bf16[128,1024]{1,0:T(8,128)(2,1)S(1)} %get-tuple-element.30), channel_id=1, source_target_pairs={{0,8},{1,9},{8,0},{9,1},{16,24},{17,25},{24,16},{25,17},{2,10},{3,... | collective-permute-start | bytes 786440 | tf_op jit(solution)/shard_map/ppermute | solution.py:280
  142.1 13.0 %collective-permute-start.13 = (bf16[128,1024]{1,0:T(8,128)(2,1)S(1)}, bf16[128,1024]{1,0:T(8,128)(2,1)S(1)}, u32[]{:S(2)}, u32[]{:S(2)}) collective-permute-start(bf16[128,1024]{1,0:T(8,128)(2,1)S(1)} %get-tuple-element.34), channel_id=1, source_target_pairs={{0,9},{1,8},{8,1},{9,0},{16,25},{17,24},{24,17},{25,16},{2,11},{3,... | collective-permute-start | bytes 786440 | tf_op jit(solution)/shard_map/ppermute | solution.py:280
  143.6 24.5 %collective-permute-start.16 = (bf16[128,1024]{1,0:T(8,128)(2,1)S(1)}, bf16[128,1024]{1,0:T(8,128)(2,1)S(1)}, u32[]{:S(2)}, u32[]{:S(2)}) collective-permute-start(bf16[128,1024]{1,0:T(8,128)(2,1)S(1)} %get-tuple-element.37), channel_id=1, source_target_pairs={{0,24},{1,25},{8,16},{9,17},{16,8},{17,9},{24,0},{25,1},{2,26},{3,... | collective-permute-start | bytes 786440 | tf_op jit(solution)/shard_map/ppermute | solution.py:280
  145.6 18.5 %collective-permute-start.14 = (bf16[128,1024]{1,0:T(8,128)(2,1)S(1)}, bf16[128,1024]{1,0:T(8,128)(2,1)S(1)}, u32[]{:S(2)}, u32[]{:S(2)}) collective-permute-start(bf16[128,1024]{1,0:T(8,128)(2,1)S(1)} %get-tuple-element.40), channel_id=1, source_target_pairs={{0,16},{1,17},{8,24},{9,25},{16,0},{17,1},{24,8},{25,9},{2,18},{3,... | collective-permute-start | bytes 786440 | tf_op jit(solution)/shard_map/ppermute | solution.py:280
  146.5 21.5 %collective-permute-start.15 = (bf16[128,1024]{1,0:T(8,128)(2,1)S(1)}, bf16[128,1024]{1,0:T(8,128)(2,1)S(1)}, u32[]{:S(2)}, u32[]{:S(2)}) collective-permute-start(bf16[128,1024]{1,0:T(8,128)(2,1)S(1)} %get-tuple-element.41), channel_id=1, source_target_pairs={{0,17},{1,16},{8,25},{9,24},{16,1},{17,0},{24,9},{25,8},{2,19},{3,... | collective-permute-start | bytes 786440 | tf_op jit(solution)/shard_map/ppermute | solution.py:280
  151.3 20.4 %collective-permute-start.17 = (bf16[128,1024]{1,0:T(8,128)(2,1)S(1)}, bf16[128,1024]{1,0:T(8,128)(2,1)S(1)}, u32[]{:S(2)}, u32[]{:S(2)}) collective-permute-start(bf16[128,1024]{1,0:T(8,128)(2,1)S(1)} %get-tuple-element.42), channel_id=1, source_target_pairs={{0,25},{1,24},{8,17},{9,16},{16,9},{17,8},{24,1},{25,0},{2,27},{3,... | collective-permute-start | bytes 786440 | tf_op jit(solution)/shard_map/ppermute | solution.py:280
  168.1 3.7 %copy-start.8 = (bf16[1,128,8192]{2,1,0:T(8,128)(2,1)}, bf16[1,128,8192]{2,1,0:T(8,128)(2,1)S(1)}, u32[]{:S(2)}) copy-start(bf16[1,128,8192]{2,1,0:T(8,128)(2,1)S(1)} %bitcast_dynamic-update-slice_fusion.1) | copy-start | bytes 6291460

commit v3 on v2

--- a/solution.py
+++ b/solution.py
@@ -43,9 +43,9 @@
             return taken
 
         queries = take(chunks)
-        states = take(chunks) if kind == "close" else []
         owns = take(4) if kind == "open" else []
         sibs = take(1) if kind == "close" else []
+        states = take(chunks) if kind == "close" else []
         kbuf, vbuf = take(2) if kind != "open" else (None, None)
         outs = take(chunks)
         if kind != "full":
@@ -56,7 +56,7 @@
         step = pl.program_id(0)
         chunk_z, chunk_core, y = plan[0, step], plan[1, step], plan[2, step]
 
-        def fill():
+        def copies_in():
             pairs = []
             for r, own in enumerate(owns):
                 here = pl.ds(OWN0 + 8 * r, 8)
@@ -68,16 +68,20 @@
                 here = pl.ds(SIB0 + 2 * slot, 2)
                 pairs.append((source.at[:, pl.ds(0, TOK)], kbuf.at[here]))
                 pairs.append((source.at[:, pl.ds(TOK, HD)], vbuf.at[here, pl.ds(0, HD)]))
-            copies = [pltpu.make_async_copy(a, b, sem.at[i]) for i, (a, b) in enumerate(pairs)]
-            for copy in copies:
+            return [pltpu.make_async_copy(a, b, sem.at[i]) for i, (a, b) in enumerate(pairs)]
+
+        def begin():
+            for copy in copies_in():
                 copy.start()
+
+        def fill():
             if owns:
                 row = lax.broadcasted_iota(jnp.int32, (VROWS - HD, TOK), 0)
                 ones = jnp.where(row == 0, 1.0, 0.0).astype(jnp.bfloat16)
                 for t in range(DUMMY):
                     vbuf[t, HD:VROWS, :] = ones
                 vbuf[DUMMY] = jnp.zeros((VROWS, TOK), jnp.bfloat16)
-            for copy in copies:
+            for copy in copies_in():
                 copy.wait()
             for r in range(len(owns)):
                 kbuf[r] = past[r, :, 0:PAST].reshape(TOK, HD)
@@ -86,7 +90,7 @@
                 kbuf[DUMMY] = kbuf[0]
 
         if kind != "full":
-            pl.when(step == 0)(fill)
+            pl.when(step == 0)(begin)
 
         def load(ref):
             for h in range(KVH):
@@ -104,6 +108,9 @@
                 if kind == "close":
                     acc[...] = states[i][0:VROWS]
                     top[...] = states[i][VROWS : VROWS + 1]
+
+        if kind != "full":
+            pl.when(step == 0)(fill)
 
         n = jnp.int32(0)
         if has_own:
@@ -229,9 +236,10 @@
     def whole(a):
         return pl.BlockSpec(a.shape, lambda i, plan: (0,) * a.ndim, pipeline_mode=pl.Buffered(1))
 
-    blocked = [*queries, *(states if kind == "close" else ())]
+    blocked = list(queries)
+    states = states if kind == "close" else []
     raw = list(source) if kind != "full" else []
-    kept = list(buffers) if kind != "open" else []
+    kept = [*states, *buffers] if kind != "open" else []
     if kind == "open":
         result = jax.ShapeDtypeStruct((VROWS + 8, GROUP), jnp.float32)
     else:
@@ -252,7 +260,7 @@
         scratch.append(pltpu.VMEM((4, 8, 2 * PAST, HD), jnp.bfloat16))
     if kind != "full":
         scratch.append(pltpu.SemaphoreType.DMA((16,)))
-    first_kept = 1 + len(blocked) + len(raw)
+    first_kept = 1 + len(blocked) + len(raw) + len(states)
     aliases = {first_kept: chunks, first_kept + 1: chunks + 1} if kind == "close" else {}
     return pl.pallas_call(
         make_kernel(kind, chunks),
@@ -263,7 +271,8 @@
             in_specs=[whole(a) for a in blocked]
             + [pl.BlockSpec(memory_space=pltpu.HBM)] * len(raw)
             + [resident] * len(kept),
-            out_specs=[pl.BlockSpec(result.shape, lambda i, plan: (0, 0))] * chunks + [resident] * len(tiles),
+            out_specs=[resident if kind == "open" else pl.BlockSpec(result.shape, lambda i, plan: (0, 0))] * chunks
+            + [resident] * len(tiles),
             scratch_shapes=scratch,
         ),
         input_output_aliases=aliases,
@@ -298,28 +307,36 @@
     return pl.pallas_call(packing, out_shape=shape, name="packing")(*arrays)
 
 
-def picking(where, own0, own1, own2, own3, out_ref):
+def picking(where, own0, own1, own2, own3, out_ref, sem):
     count = out_ref.shape[0]
+
+    def copy(own, e):
+        pair = own.at[pl.ds(2 * where[count + e], 2), pl.ds(0, TOK + HD)]
+        return pltpu.make_async_copy(pair, out_ref.at[e], sem.at[e])
+
     for e in range(count):
         for r, own in enumerate((own0, own1, own2, own3)):
 
             @pl.when(where[e] == r)
             def _(own=own, e=e):
-                out_ref[e] = own[pl.ds(2 * where[count + e], 2), 0 : TOK + HD]
+                copy(own, e).start()
+
+    for e in range(count):
+        copy(own0, e).wait()
 
 
 def picked(where, owns):
     entries = where.shape[0] // 2
     shape = (entries, 2, TOK + HD, HD)
-    whole = pl.BlockSpec(owns[0].shape, lambda i, where: (0, 0, 0), pipeline_mode=pl.Buffered(1))
     return pl.pallas_call(
         picking,
         out_shape=jax.ShapeDtypeStruct(shape, jnp.bfloat16),
         grid_spec=pltpu.PrefetchScalarGridSpec(
             num_scalar_prefetch=1,
             grid=(1,),
-            in_specs=[whole] * 4,
+            in_specs=[pl.BlockSpec(memory_space=pltpu.HBM)] * 4,
             out_specs=pl.BlockSpec(shape, lambda i, where: (0, 0, 0, 0), pipeline_mode=pl.Buffered(1)),
+            scratch_shapes=[pltpu.SemaphoreType.DMA((entries,))],
         ),
         compiler_params=pltpu.CompilerParams(vmem_limit_bytes=16 * 2**20),
         name="picking",
@@ -333,17 +350,6 @@
 
     send = packed(key_new, value_new, hist_key, hist_value)
     own = lax.all_to_all(send, (Z, CORE), split_axis=0, concat_axis=0, tiled=True)
-    up, down = shifted(own, Y, 1), shifted(own, Y, -1)
-    onward = shifted(up[:4], Y, 1), shifted(down[4:], Y, -1)
-    over = jnp.concatenate(onward, axis=0)
-    owns = (own, up, over, down)
-
-    cols = after(query[0], own)
-    queries = {}
-    for s in QORDER:
-        piece = lax.dynamic_slice_in_dim(cols, (me ^ s) * GROUP, GROUP, 1)
-        queries[s] = exchanged(piece, s) if s else piece
-
     my_source = lax.dynamic_index_in_dim(sib_source, reader, 0, keepdims=False)
     my_mask = lax.dynamic_index_in_dim(sib_mask, reader, 0, keepdims=False)
     from_me = sib_source == reader
@@ -353,8 +359,6 @@
     )
     send_table = jnp.sum(jnp.where(slot_hit, sib_block[:, :, None], 0), axis=1).reshape(-1)
     where = jnp.concatenate([(y - send_table) % 4, send_table // 4]).astype(jnp.int32)
-    sent = picked(where, owns)
-    sib = lax.all_to_all(sent, "branch", split_axis=0, concat_axis=0, tiled=True)
     slots = jnp.arange(NSIB, dtype=jnp.int32)
     same = (my_source[None, :] == my_source[:, None]) & (slots[None, :] < slots[:, None])
     rank = jnp.sum(same.astype(jnp.int32), axis=1)
@@ -367,13 +371,28 @@
         rows.append(jnp.broadcast_to(flat[:, None], (NSIB, len(steps))))
         return jnp.concatenate(rows, axis=0).astype(jnp.int32)
 
+    plans = [plan_of(steps) for _, steps in CALLS]
+    own, where, *plans = lax.optimization_barrier((own, where, *plans))
+    up, down = shifted(own, Y, 1), shifted(own, Y, -1)
+    onward = shifted(up[:4], Y, 1), shifted(down[4:], Y, -1)
+    over = jnp.concatenate(onward, axis=0)
+    owns = (own, up, over, down)
+
+    cols = after(query[0], own)
+    queries = {}
+    for s in QORDER:
+        piece = lax.dynamic_slice_in_dim(cols, (me ^ s) * GROUP, GROUP, 1)
+        queries[s] = exchanged(piece, s) if s else piece
+
+    sent = picked(where, owns)
+    sib = lax.all_to_all(sent, "branch", split_axis=0, concat_axis=0, tiled=True)
     parts, states, previous, buffers = {}, {}, None, ()
-    for kind, steps in CALLS:
+    for number, (kind, steps) in enumerate(CALLS):
         asked = [queries[s] for s in steps]
         if previous is not None:
             asked[0] = after(asked[0], previous)
         source = owns if kind == "open" else (sib,)
-        results = attend(kind, plan_of(steps), asked, [states.get(s) for s in steps], source, buffers)
+        results = attend(kind, plans[number], asked, [states.get(s) for s in steps], source, buffers)
         if kind != "full":
             buffers = results[len(steps) :]
         previous = results[0]

time: 173 us -> 172 us (level)
  local copies, waits for them, and re-layouts: 8.15 us -> 11.2 us
  waiting for transfers between devices: 61.4 us -> 58.7 us
    all_to_all x1, waiting for transfers between devices: 10.5 us -> 7.11 us  [attention(): lax.all_to_all(send, (Z, CORE), split_axis=0, concat_axis=0, tiled=True)]
    unnamed x25 -> x31, local copies, waits for them, and re-layouts: 2.52 us -> 5.4 us
  transfers between devices with their start and end apart: 20 -> 20, of which waited for: 11 -> 11; matrix products, arithmetic and copies ran while one was open for 3% -> 3% of each run, Pallas kernels for 31% -> 30%
where the time goes in v3:
time: 172 us; the launch traced here: 171 us
  Pallas kernels  71.5 us (42%)
  waiting for transfers between devices  58.7 us (34%)
  starting transfers between devices  28.6 us (17%)
  local copies, waits for them, and re-layouts  11.2 us (7%)
    pallas_call x5, Pallas kernels, attend(): pl.pallas_call(make_kernel(kind, chunks), out_shape=(result,) * chunks +...  66.3 us
    ppermute x14, waiting for transfers between devices, exchanged(): return lax.ppermute(value, (Z, CORE), [(k, k ^ step) for k in range(8)])  30.8 us
    ppermute x4, waiting for transfers between devices, shifted(): return lax.ppermute(value, axis, [(k, (k + by) % n) for k in range(n)])  20.8 us
    ppermute x14, starting transfers between devices, exchanged(): return lax.ppermute(value, (Z, CORE), [(k, k ^ step) for k in range(8)])  14.5 us
    all_to_all x1, waiting for transfers between devices, attention(): lax.all_to_all(send, (Z, CORE), split_axis=0, concat_axis=0, tiled=True)  7.11 us
    unnamed x31, local copies, waits for them, and re-layouts  5.4 us
    all_to_all x1, starting transfers between devices, attention(): lax.all_to_all(send, (Z, CORE), split_axis=0, concat_axis=0, tiled=True)  5.31 us
    all_to_all x1, starting transfers between devices, attention(): lax.all_to_all(sent, 'branch', split_axis=0, concat_axis=0, tiled=True)  4.54 us
  transfers between devices with their start and end apart: 20, of which 11 were waited for; matrix products, arithmetic and copies ran while one was open for 3% of the time, Pallas kernels for 30%

profile of v3, /device:TPU:30, one launch (start us, length us, event | category | flops | bytes accessed | tf_op | source)
XLA Modules:
  0.0 171.2 jit_solution(13100748588885690418)
XLA Ops:
  0.0 2.0 %packing.1 = bf16[8,288,128]{2,1,0:T(8,128)(2,1)} custom-call(bf16[1,128,1024]{2,1,0:T(8,128)(2,1)} %key_ref.1, bf16[1,128,1024]{2,1,0:T(8,128)(2,1)} %value_ref.1, bf16[16,1024]{1,0:T(8,128)(2,1)} %past_key_ref.1, bf16[16,1024]{1,0:T(8,128)(2,1)} %past_value_ref.1), custom_call_target="tpu_custom_call" | custom-call | tf_op jit(solution)/shard_map/packing/pallas_call | solution.py:307
  2.0 5.3 %all-to-all-start = ((bf16[8,288,128]{2,1,0:T(8,128)(2,1)}), bf16[8,288,128]{2,1,0:T(8,128)(2,1)S(1)}, u32[]{:S(2)}, u32[]{:S(2)}) async-start(bf16[8,288,128]{2,1,0:T(8,128)(2,1)} %packing.1), calls=%async_computation | async-start | bytes 1179648 | tf_op jit(solution)/shard_map/all_to_all | solution.py:352
  11.2 7.1 %all-to-all-done.refs_2_.own0 = bf16[8,288,128]{2,1,0:T(8,128)(2,1)S(1)} async-done(((bf16[8,288,128]{2,1,0:T(8,128)(2,1)}), bf16[8,288,128]{2,1,0:T(8,128)(2,1)S(1)}, u32[]{:S(2)}, u32[]{:S(2)}) %all-to-all-start) | async-done | bytes 589856 | tf_op jit(solution)/shard_map/all_to_all | solution.py:352
  18.6 1.8 %collective-permute-start.6 = (bf16[8,288,128]{2,1,0:T(8,128)(2,1)S(1)}, bf16[8,288,128]{2,1,0:T(8,128)(2,1)S(1)}, u32[]{:S(2)}, u32[]{:S(2)}) collective-permute-start(bf16[8,288,128]{2,1,0:T(8,128)(2,1)S(1)} %all-to-all-done.refs_2_.own0), channel_id=1, source_target_pairs={{0,6},{2,0},{4,2},{6,4},{1,7},{3,1},{5,3},{7,5},{8,14},{10,8},{12,... | collective-permute-start | bytes 1769480 | tf_op jit(solution)/shard_map/ppermute | solution.py:285
  20.4 12.7 %collective-permute-done.4.refs_3_.own1 = bf16[8,288,128]{2,1,0:T(8,128)(2,1)S(1)} collective-permute-done((bf16[8,288,128]{2,1,0:T(8,128)(2,1)S(1)}, bf16[8,288,128]{2,1,0:T(8,128)(2,1)S(1)}, u32[]{:S(2)}, u32[]{:S(2)}) %collective-permute-start.4) | collective-permute-done | bytes 589856 | tf_op jit(solution)/shard_map/ppermute | solution.py:285
  33.1 1.6 collective-permute-start.5
  35.3 5.5 %collective-permute-done.5 = bf16[4,288,128]{2,1,0:T(8,128)(2,1)S(1)} collective-permute-done((bf16[4,288,128]{2,1,0:T(8,128)(2,1)S(1)}, bf16[4,288,128]{2,1,0:T(8,128)(2,1)S(1)}, u32[]{:S(2)}, u32[]{:S(2)}) %collective-permute-start.5) | collective-permute-done | bytes 294944 | tf_op jit(solution)/shard_map/ppermute | solution.py:285
  40.8 2.6 %collective-permute-done.7 = bf16[4,288,128]{2,1,0:T(8,128)(2,1)S(1)} collective-permute-done((bf16[4,288,128]{2,1,0:T(8,128)(2,1)S(1)}, bf16[4,288,128]{2,1,0:T(8,128)(2,1)S(1)}, u32[]{:S(2)}, u32[]{:S(2)}) %collective-permute-start.7) | collective-permute-done | bytes 294944 | tf_op jit(solution)/shard_map/ppermute | solution.py:285
  44.3 3.2 %picking.1 = bf16[8,2,256,128]{3,2,1,0:T(8,128)(2,1)} custom-call(s32[16]{0:T(128)S(1)} %pad_add_fusion.4.where, bf16[8,288,128]{2,1,0:T(8,128)(2,1)} %copy-done.5, bf16[8,288,128]{2,1,0:T(8,128)(2,1)} %copy-done.6, bf16[8,288,128]{2,1,0:T(8,128)(2,1)} %copy-done.8, bf16[8,288,128]{2,1,0:T(8,128)(2,1)} %copy-done.7), custom_call_target="tpu_custom_call" | custom-call | tf_op jit(solution)/shard_map/picking/pallas_call | solution.py:331
  47.5 4.5 %all-to-all-start.1 = ((bf16[8,2,256,128]{3,2,1,0:T(8,128)(2,1)}), bf16[8,2,256,128]{3,2,1,0:T(8,128)(2,1)}, u32[]{:S(2)}, u32[]{:S(2)}) async-start(bf16[8,2,256,128]{3,2,1,0:T(8,128)(2,1)} %picking.1), calls=%async_computation.1 | async-start | bytes 2097152 | tf_op jit(solution)/shard_map/all_to_all | solution.py:388
  52.0 1.2 constant_dynamic-slice_fusion
  53.8 2.1 %collective-permute-start.3 = (bf16[128,1024]{1,0:T(8,128)(2,1)S(1)}, bf16[128,1024]{1,0:T(8,128)(2,1)S(1)}, u32[]{:S(2)}, u32[]{:S(2)}) collective-permute-start(bf16[128,1024]{1,0:T(8,128)(2,1)S(1)} %get-tuple-element.63), channel_id=1, source_target_pairs={{0,16},{1,17},{8,24},{9,25},{16,0},{17,1},{24,8},{25,9},{2,18},{3,... | collective-permute-start | bytes 786440 | tf_op jit(solution)/shard_map/ppermute | solution.py:289
  55.9 3.2 %collective-permute-start.8 = (bf16[128,1024]{1,0:T(8,128)(2,1)}, bf16[128,1024]{1,0:T(8,128)(2,1)}, u32[]{:S(2)}, u32[]{:S(2)}) collective-permute-start(bf16[128,1024]{1,0:T(8,128)(2,1)} %get-tuple-element.62), channel_id=1, source_target_pairs={{0,17},{1,16},{8,25},{9,24},{16,1},{17,0},{24,9},{25,8},{2,19},{3,... | collective-permute-start | bytes 786440 | tf_op jit(solution)/shard_map/ppermute | solution.py:289
  59.1 1.2 collective-permute-start
  60.3 2.1 %collective-permute-done.2.refs_0_ = bf16[128,1024]{1,0:T(8,128)(2,1)S(1)} collective-permute-done((bf16[128,1024]{1,0:T(8,128)(2,1)S(1)}, bf16[128,1024]{1,0:T(8,128)(2,1)S(1)}, u32[]{:S(2)}, u32[]{:S(2)}) %collective-permute-start.2) | collective-permute-done | bytes 262176 | tf_op jit(solution)/shard_map/ppermute | solution.py:289
  62.4 6.3 %collective-permute-done.3.refs_1_ = bf16[128,1024]{1,0:T(8,128)(2,1)S(1)} collective-permute-done((bf16[128,1024]{1,0:T(8,128)(2,1)S(1)}, bf16[128,1024]{1,0:T(8,128)(2,1)S(1)}, u32[]{:S(2)}, u32[]{:S(2)}) %collective-permute-start.3) | collective-permute-done | bytes 262176 | tf_op jit(solution)/shard_map/ppermute | solution.py:289
  69.9 14.2 %shard_map.82 = (f32[152,1024]{1,0:T(8,128)S(1)}, f32[152,1024]{1,0:T(8,128)S(1)}, bf16[45,128,128]{2,1,0:T(8,128)(2,1)S(1)}, bf16[45,144,128]{2,1,0:T(8,128)(2,1)S(1)}) custom-call(s32[11,2]{1,0:T(8,128)S(1)} %copy.41.plan, bf16[128,1024]{1,0:T(8,128)(2,1)} %copy-done.11, bf16[128,1024]{1,0:T(8,128)(2,1)} %copy-done.12, bf16[8,288,128]{2,1,0:T(8,128)(2,1)} %copy-done.5, ...), custom_call_target="tpu_custom_call" | custom-call | tf_op jit(solution)/shard_map/pallas_call | solution.py:265
  84.2 0.8 copy-done.1
  85.9 1.1 copy-done.2
  86.9 1.1 copy-done.4
  88.0 7.3 %shard_map.83 = (bf16[128,1024]{1,0:T(8,128)(2,1)S(1)}, bf16[128,1024]{1,0:T(8,128)(2,1)S(1)}, bf16[45,128,128]{2,1,0:T(8,128)(2,1)S(1)}, bf16[45,144,128]{2,1,0:T(8,128)(2,1)S(1)}) custom-call(s32[11,2]{1,0:T(8,128)S(1)} %copy.42.plan, bf16[128,1024]{1,0:T(8,128)(2,1)} %copy-done.11, ...), custom_call_target="tpu_custom_call", output_to_operand_aliasing={{2}: (6, {}), {3}: (7, {})} | custom-call | tf_op jit(solution)/shard_map/pallas_call | solution.py:265
  95.3 16.0 %shard_map.84 = (bf16[128,1024]{1,0:T(8,128)(2,1)S(1)}, bf16[128,1024]{1,0:T(8,128)(2,1)S(1)}) custom-call(s32[11,2]{1,0:T(8,128)S(1)} %copy.43.plan, bf16[128,1024]{1,0:T(8,128)(2,1)} %collective-permute-done.1.refs_0_, bf16[128,1024]{1,0:T(8,128)(2,1)} %collective-permute-done.8.refs_1_, bf16[45,128,128]{2,1,0:T(8,128)(2,1)S(1)} %get-tuple-element.45.refs_2_, ...), custom_call_target="tpu_custom_call" | custom-call | tf_op jit(solution)/shard_map/pallas_call | solution.py:265
  111.3 14.4 %shard_map.85 = (bf16[128,1024]{1,0:T(8,128)(2,1)S(1)}, bf16[128,1024]{1,0:T(8,128)(2,1)S(1)}) custom-call(s32[11,2]{1,0:T(8,128)S(1)} %copy.44.plan, bf16[128,1024]{1,0:T(8,128)(2,1)} %collective-permute-done.refs_0_, bf16[128,1024]{1,0:T(8,128)(2,1)} %get-tuple-element.61.refs_1_, bf16[45,128,128]{2,1,0:T(8,128)(2,1)S(1)} %get-tuple-element.45.refs_2_, ...), custom_call_target="tpu_custom_call" | custom-call | tf_op jit(solution)/shard_map/pallas_call | solution.py:265
  125.8 14.4 %shard_map.86 = (bf16[128,1024]{1,0:T(8,128)(2,1)S(1)}, bf16[128,1024]{1,0:T(8,128)(2,1)S(1)}) custom-call(s32[11,2]{1,0:T(8,128)S(1)} %copy.45.plan, bf16[128,1024]{1,0:T(8,128)(2,1)} %collective-permute-done.9.refs_0_, bf16[128,1024]{1,0:T(8,128)(2,1)} %collective-permute-done.10.refs_1_, bf16[45,128,128]{2,1,0:T(8,128)(2,1)S(1)} %get-tuple-element.45.refs_2_, ...), custom_call_target="tpu_custom_call" | custom-call | tf_op jit(solution)/shard_map/pallas_call | solution.py:265
  140.9 1.4 collective-permute-start.13
  142.3 2.0 %collective-permute-start.16 = (bf16[128,1024]{1,0:T(8,128)(2,1)S(1)}, bf16[128,1024]{1,0:T(8,128)(2,1)S(1)}, u32[]{:S(2)}, u32[]{:S(2)}) collective-permute-start(bf16[128,1024]{1,0:T(8,128)(2,1)S(1)} %get-tuple-element.51), channel_id=1, source_target_pairs={{0,24},{1,25},{8,16},{9,17},{16,8},{17,9},{24,0},{25,1},{2,26},{3,... | collective-permute-start | bytes 786440 | tf_op jit(solution)/shard_map/ppermute | solution.py:289
  145.2 2.7 %collective-permute-start.15 = (bf16[128,1024]{1,0:T(8,128)(2,1)S(1)}, bf16[128,1024]{1,0:T(8,128)(2,1)S(1)}, u32[]{:S(2)}, u32[]{:S(2)}) collective-permute-start(bf16[128,1024]{1,0:T(8,128)(2,1)S(1)} %get-tuple-element.55), channel_id=1, source_target_pairs={{0,17},{1,16},{8,25},{9,24},{16,1},{17,0},{24,9},{25,8},{2,19},{3,... | collective-permute-start | bytes 786440 | tf_op jit(solution)/shard_map/ppermute | solution.py:289
  147.9 2.1 %collective-permute-done.12 = bf16[128,1024]{1,0:T(8,128)(2,1)S(1)} collective-permute-done((bf16[128,1024]{1,0:T(8,128)(2,1)S(1)}, bf16[128,1024]{1,0:T(8,128)(2,1)S(1)}, u32[]{:S(2)}, u32[]{:S(2)}) %collective-permute-start.12) | collective-permute-done | bytes 262176 | tf_op jit(solution)/shard_map/ppermute | solution.py:289
  150.1 3.8 %collective-permute-done.13 = bf16[128,1024]{1,0:T(8,128)(2,1)S(1)} collective-permute-done((bf16[128,1024]{1,0:T(8,128)(2,1)S(1)}, bf16[128,1024]{1,0:T(8,128)(2,1)S(1)}, u32[]{:S(2)}, u32[]{:S(2)}) %collective-permute-start.13) | collective-permute-done | bytes 262176 | tf_op jit(solution)/shard_map/ppermute | solution.py:289
  153.9 8.9 %collective-permute-done.14 = bf16[128,1024]{1,0:T(8,128)(2,1)S(1)} collective-permute-done((bf16[128,1024]{1,0:T(8,128)(2,1)S(1)}, bf16[128,1024]{1,0:T(8,128)(2,1)S(1)}, u32[]{:S(2)}, u32[]{:S(2)}) %collective-permute-start.14) | collective-permute-done | bytes 262176 | tf_op jit(solution)/shard_map/ppermute | solution.py:289
  162.8 3.8 %collective-permute-done.15 = bf16[128,1024]{1,0:T(8,128)(2,1)S(1)} collective-permute-done((bf16[128,1024]{1,0:T(8,128)(2,1)S(1)}, bf16[128,1024]{1,0:T(8,128)(2,1)S(1)}, u32[]{:S(2)}, u32[]{:S(2)}) %collective-permute-start.15) | collective-permute-done | bytes 262176 | tf_op jit(solution)/shard_map/ppermute | solution.py:289
  166.8 3.7 %collective-permute-done.17 = bf16[128,1024]{1,0:T(8,128)(2,1)S(1)} collective-permute-done((bf16[128,1024]{1,0:T(8,128)(2,1)S(1)}, bf16[128,1024]{1,0:T(8,128)(2,1)S(1)}, u32[]{:S(2)}, u32[]{:S(2)}) %collective-permute-start.17) | collective-permute-done | bytes 262176 | tf_op jit(solution)/shard_map/ppermute | solution.py:289
  (97 shorter events, 10.6 us)
Async XLA Ops:
  0.0 7.5 %copy-start = (s32[4,16,4]{1,2,0:T(4,128)S(1)}, s32[4,16,4]{1,2,0:T(4,128)}, u32[]{:S(2)}) copy-start(s32[4,16,4]{1,2,0:T(4,128)} %param.15) | copy-start | bytes 3076
  0.0 7.5 %copy-start.13 = (s32[4,4]{1,0:T(4,128)S(1)}, s32[4,4]{1,0:T(4,128)}, u32[]{:S(2)}) copy-start(s32[4,4]{1,0:T(4,128)} %param.13) | copy-start | bytes 196
  0.0 10.4 %copy-start.14 = (s32[4,4]{1,0:T(4,128)S(1)}, s32[4,4]{1,0:T(4,128)}, u32[]{:S(2)}) copy-start(s32[4,4]{1,0:T(4,128)} %param.14) | copy-start | bytes 196
  2.0 16.3 %all-to-all-start = ((bf16[8,288,128]{2,1,0:T(8,128)(2,1)}), bf16[8,288,128]{2,1,0:T(8,128)(2,1)S(1)}, u32[]{:S(2)}, u32[]{:S(2)}) async-start(bf16[8,288,128]{2,1,0:T(8,128)(2,1)} %packing.1), calls=%async_computation | async-start | bytes 1179648 | tf_op jit(solution)/shard_map/all_to_all | solution.py:352
  18.3 25.1 %copy-start.5 = (bf16[8,288,128]{2,1,0:T(8,128)(2,1)}, bf16[8,288,128]{2,1,0:T(8,128)(2,1)S(1)}, u32[]{:S(2)}) copy-start(bf16[8,288,128]{2,1,0:T(8,128)(2,1)S(1)} %all-to-all-done.refs_2_.own0) | copy-start | bytes 1769476
  18.3 14.8 %collective-permute-start.4 = (bf16[8,288,128]{2,1,0:T(8,128)(2,1)S(1)}, bf16[8,288,128]{2,1,0:T(8,128)(2,1)S(1)}, u32[]{:S(2)}, u32[]{:S(2)}) collective-permute-start(bf16[8,288,128]{2,1,0:T(8,128)(2,1)S(1)} %all-to-all-done.refs_2_.own0), channel_id=1, source_target_pairs={{0,2},{2,4},{4,6},{6,0},{1,3},{3,5},{5,7},{7,1},{8,10},{10,12},{12... | collective-permute-start | bytes 1769480 | tf_op jit(solution)/shard_map/ppermute | solution.py:285
  18.6 16.1 %collective-permute-start.6 = (bf16[8,288,128]{2,1,0:T(8,128)(2,1)S(1)}, bf16[8,288,128]{2,1,0:T(8,128)(2,1)S(1)}, u32[]{:S(2)}, u32[]{:S(2)}) collective-permute-start(bf16[8,288,128]{2,1,0:T(8,128)(2,1)S(1)} %all-to-all-done.refs_2_.own0), channel_id=1, source_target_pairs={{0,6},{2,0},{4,2},{6,4},{1,7},{3,1},{5,3},{7,5},{8,14},{10,8},{12,... | collective-permute-start | bytes 1769480 | tf_op jit(solution)/shard_map/ppermute | solution.py:285
  33.1 10.3 %copy-start.6 = (bf16[8,288,128]{2,1,0:T(8,128)(2,1)}, bf16[8,288,128]{2,1,0:T(8,128)(2,1)S(1)}, u32[]{:S(2)}) copy-start(bf16[8,288,128]{2,1,0:T(8,128)(2,1)S(1)} %collective-permute-done.4.refs_3_.own1) | copy-start | bytes 1769476
  33.1 7.7 %collective-permute-start.5 = (bf16[4,288,128]{2,1,0:T(8,128)(2,1)S(1)}, bf16[4,288,128]{2,1,0:T(8,128)(2,1)S(1)}, u32[]{:S(2)}, u32[]{:S(2)}) collective-permute-start(bf16[4,288,128]{2,1,0:T(8,128)(2,1)S(1)} %slice.16), channel_id=1, source_target_pairs={{0,2},{2,4},{4,6},{6,0},{1,3},{3,5},{5,7},{7,1},{8,10},{10,12},{12... | collective-permute-start | bytes 884744 | tf_op jit(solution)/shard_map/ppermute | solution.py:285
  34.7 8.7 %copy-start.7 = (bf16[8,288,128]{2,1,0:T(8,128)(2,1)}, bf16[8,288,128]{2,1,0:T(8,128)(2,1)S(1)}, u32[]{:S(2)}) copy-start(bf16[8,288,128]{2,1,0:T(8,128)(2,1)S(1)} %collective-permute-done.6.refs_5_.own3) | copy-start | bytes 1769476
  34.7 8.7 %collective-permute-start.7 = (bf16[4,288,128]{2,1,0:T(8,128)(2,1)S(1)}, bf16[4,288,128]{2,1,0:T(8,128)(2,1)S(1)}, u32[]{:S(2)}, u32[]{:S(2)}) collective-permute-start(bf16[4,288,128]{2,1,0:T(8,128)(2,1)S(1)} %slice.17), channel_id=1, source_target_pairs={{0,6},{2,0},{4,2},{6,4},{1,7},{3,1},{5,3},{7,5},{8,14},{10,8},{12,... | collective-permute-start | bytes 884744 | tf_op jit(solution)/shard_map/ppermute | solution.py:285
  44.3 7.7 %copy-start.9 = (bf16[1,128,8192]{2,1,0:T(8,128)(2,1)S(1)}, bf16[1,128,8192]{2,1,0:T(8,128)(2,1)}, u32[]{:S(2)}) copy-start(bf16[1,128,8192]{2,1,0:T(8,128)(2,1)} %param.8) | copy-start | bytes 6291460
  47.5 38.4 %all-to-all-start.1 = ((bf16[8,2,256,128]{3,2,1,0:T(8,128)(2,1)}), bf16[8,2,256,128]{3,2,1,0:T(8,128)(2,1)}, u32[]{:S(2)}, u32[]{:S(2)}) async-start(bf16[8,2,256,128]{3,2,1,0:T(8,128)(2,1)} %picking.1), calls=%async_computation.1 | async-start | bytes 2097152 | tf_op jit(solution)/shard_map/all_to_all | solution.py:388
  53.3 9.2 %collective-permute-start.2 = (bf16[128,1024]{1,0:T(8,128)(2,1)S(1)}, bf16[128,1024]{1,0:T(8,128)(2,1)S(1)}, u32[]{:S(2)}, u32[]{:S(2)}) collective-permute-start(bf16[128,1024]{1,0:T(8,128)(2,1)S(1)} %get-tuple-element.64), channel_id=1, source_target_pairs={{0,8},{1,9},{8,0},{9,1},{16,24},{17,25},{24,16},{25,17},{2,10},{3,... | collective-permute-start | bytes 786440 | tf_op jit(solution)/shard_map/ppermute | solution.py:289
  53.8 14.9 %collective-permute-start.3 = (bf16[128,1024]{1,0:T(8,128)(2,1)S(1)}, bf16[128,1024]{1,0:T(8,128)(2,1)S(1)}, u32[]{:S(2)}, u32[]{:S(2)}) collective-permute-start(bf16[128,1024]{1,0:T(8,128)(2,1)S(1)} %get-tuple-element.63), channel_id=1, source_target_pairs={{0,16},{1,17},{8,24},{9,25},{16,0},{17,1},{24,8},{25,9},{2,18},{3,... | collective-permute-start | bytes 786440 | tf_op jit(solution)/shard_map/ppermute | solution.py:289
  55.9 39.4 %collective-permute-start.1 = (bf16[128,1024]{1,0:T(8,128)(2,1)}, bf16[128,1024]{1,0:T(8,128)(2,1)}, u32[]{:S(2)}, u32[]{:S(2)}) collective-permute-start(bf16[128,1024]{1,0:T(8,128)(2,1)} %get-tuple-element.65), channel_id=1, source_target_pairs={{0,9},{1,8},{8,1},{9,0},{16,25},{17,24},{24,17},{25,16},{2,11},{3,... | collective-permute-start | bytes 786440 | tf_op jit(solution)/shard_map/ppermute | solution.py:289
  55.9 39.4 %collective-permute-start.8 = (bf16[128,1024]{1,0:T(8,128)(2,1)}, bf16[128,1024]{1,0:T(8,128)(2,1)}, u32[]{:S(2)}, u32[]{:S(2)}) collective-permute-start(bf16[128,1024]{1,0:T(8,128)(2,1)} %get-tuple-element.62), channel_id=1, source_target_pairs={{0,17},{1,16},{8,25},{9,24},{16,1},{17,0},{24,9},{25,8},{2,19},{3,... | collective-permute-start | bytes 786440 | tf_op jit(solution)/shard_map/ppermute | solution.py:289
  59.1 52.2 %collective-permute-start = (bf16[128,1024]{1,0:T(8,128)(2,1)}, bf16[128,1024]{1,0:T(8,128)(2,1)}, u32[]{:S(2)}, u32[]{:S(2)}) collective-permute-start(bf16[128,1024]{1,0:T(8,128)(2,1)} %get-tuple-element.66), channel_id=1, source_target_pairs={{0,24},{1,25},{8,16},{9,17},{16,8},{17,9},{24,0},{25,1},{2,26},{3,... | collective-permute-start | bytes 786440 | tf_op jit(solution)/shard_map/ppermute | solution.py:289
  62.4 7.5 %copy-start.11 = (bf16[128,1024]{1,0:T(8,128)(2,1)}, bf16[128,1024]{1,0:T(8,128)(2,1)S(1)}, u32[]{:S(2)}) copy-start(bf16[128,1024]{1,0:T(8,128)(2,1)S(1)} %collective-permute-done.2.refs_0_) | copy-start | bytes 786436
  62.4 63.3 %collective-permute-start.9 = (bf16[128,1024]{1,0:T(8,128)(2,1)}, bf16[128,1024]{1,0:T(8,128)(2,1)}, u32[]{:S(2)}, u32[]{:S(2)}) collective-permute-start(bf16[128,1024]{1,0:T(8,128)(2,1)} %get-tuple-element.60), channel_id=1, source_target_pairs={{0,25},{1,24},{8,17},{9,16},{16,9},{17,8},{24,1},{25,0},{2,27},{3,... | collective-permute-start | bytes 786440 | tf_op jit(solution)/shard_map/ppermute | solution.py:289
  69.5 56.3 %collective-permute-start.10 = (bf16[128,1024]{1,0:T(8,128)(2,1)}, bf16[128,1024]{1,0:T(8,128)(2,1)}, u32[]{:S(2)}, u32[]{:S(2)}) collective-permute-start(bf16[128,1024]{1,0:T(8,128)(2,1)} %get-tuple-element.59), channel_id=1, source_target_pairs={{0,1},{1,0},{8,9},{9,8},{16,17},{17,16},{24,25},{25,24},{2,3},{3,2... | collective-permute-start | bytes 786440 | tf_op jit(solution)/shard_map/ppermute | solution.py:289
  84.2 0.9 copy-start.1
  85.9 1.1 copy-start.2
  86.9 1.1 copy-start.4
  140.2 5.0 %collective-permute-start.11 = (bf16[128,1024]{1,0:T(8,128)(2,1)S(1)}, bf16[128,1024]{1,0:T(8,128)(2,1)S(1)}, u32[]{:S(2)}, u32[]{:S(2)}) collective-permute-start(bf16[128,1024]{1,0:T(8,128)(2,1)S(1)} %get-tuple-element.53), channel_id=1, source_target_pairs={{0,1},{1,0},{8,9},{9,8},{16,17},{17,16},{24,25},{25,24},{2,3},{3,2... | collective-permute-start | bytes 786440 | tf_op jit(solution)/shard_map/ppermute | solution.py:289
  140.9 9.2 %collective-permute-start.12 = (bf16[128,1024]{1,0:T(8,128)(2,1)S(1)}, bf16[128,1024]{1,0:T(8,128)(2,1)S(1)}, u32[]{:S(2)}, u32[]{:S(2)}) collective-permute-start(bf16[128,1024]{1,0:T(8,128)(2,1)S(1)} %get-tuple-element.43), channel_id=1, source_target_pairs={{0,8},{1,9},{8,0},{9,1},{16,24},{17,25},{24,16},{25,17},{2,10},{3,... | collective-permute-start | bytes 786440 | tf_op jit(solution)/shard_map/ppermute | solution.py:289
  140.9 13.0 %collective-permute-start.13 = (bf16[128,1024]{1,0:T(8,128)(2,1)S(1)}, bf16[128,1024]{1,0:T(8,128)(2,1)S(1)}, u32[]{:S(2)}, u32[]{:S(2)}) collective-permute-start(bf16[128,1024]{1,0:T(8,128)(2,1)S(1)} %get-tuple-element.47), channel_id=1, source_target_pairs={{0,9},{1,8},{8,1},{9,0},{16,25},{17,24},{24,17},{25,16},{2,11},{3,... | collective-permute-start | bytes 786440 | tf_op jit(solution)/shard_map/ppermute | solution.py:289
  142.3 24.4 %collective-permute-start.16 = (bf16[128,1024]{1,0:T(8,128)(2,1)S(1)}, bf16[128,1024]{1,0:T(8,128)(2,1)S(1)}, u32[]{:S(2)}, u32[]{:S(2)}) collective-permute-start(bf16[128,1024]{1,0:T(8,128)(2,1)S(1)} %get-tuple-element.51), channel_id=1, source_target_pairs={{0,24},{1,25},{8,16},{9,17},{16,8},{17,9},{24,0},{25,1},{2,26},{3,... | collective-permute-start | bytes 786440 | tf_op jit(solution)/shard_map/ppermute | solution.py:289
  144.3 18.5 %collective-permute-start.14 = (bf16[128,1024]{1,0:T(8,128)(2,1)S(1)}, bf16[128,1024]{1,0:T(8,128)(2,1)S(1)}, u32[]{:S(2)}, u32[]{:S(2)}) collective-permute-start(bf16[128,1024]{1,0:T(8,128)(2,1)S(1)} %get-tuple-element.54), channel_id=1, source_target_pairs={{0,16},{1,17},{8,24},{9,25},{16,0},{17,1},{24,8},{25,9},{2,18},{3,... | collective-permute-start | bytes 786440 | tf_op jit(solution)/shard_map/ppermute | solution.py:289
  145.2 21.5 %collective-permute-start.15 = (bf16[128,1024]{1,0:T(8,128)(2,1)S(1)}, bf16[128,1024]{1,0:T(8,128)(2,1)S(1)}, u32[]{:S(2)}, u32[]{:S(2)}) collective-permute-start(bf16[128,1024]{1,0:T(8,128)(2,1)S(1)} %get-tuple-element.55), channel_id=1, source_target_pairs={{0,17},{1,16},{8,25},{9,24},{16,1},{17,0},{24,9},{25,8},{2,19},{3,... | collective-permute-start | bytes 786440 | tf_op jit(solution)/shard_map/ppermute | solution.py:289
  150.0 20.4 %collective-permute-start.17 = (bf16[128,1024]{1,0:T(8,128)(2,1)S(1)}, bf16[128,1024]{1,0:T(8,128)(2,1)S(1)}, u32[]{:S(2)}, u32[]{:S(2)}) collective-permute-start(bf16[128,1024]{1,0:T(8,128)(2,1)S(1)} %get-tuple-element.56), channel_id=1, source_target_pairs={{0,25},{1,24},{8,17},{9,16},{16,9},{17,8},{24,1},{25,0},{2,27},{3,... | collective-permute-start | bytes 786440 | tf_op jit(solution)/shard_map/ppermute | solution.py:289
  166.7 3.7 %copy-start.10 = (bf16[1,128,8192]{2,1,0:T(8,128)(2,1)}, bf16[1,128,8192]{2,1,0:T(8,128)(2,1)S(1)}, u32[]{:S(2)}) copy-start(bf16[1,128,8192]{2,1,0:T(8,128)(2,1)S(1)} %bitcast_dynamic-update-slice_fusion.1) | copy-start | bytes 6291460
  (3 other events, 2.4 us)
